TPU v7x, 32 devices: a whole 2x2x4 slice. The times are simulated.
32 devices in a mesh: wide: 8 (over z, y), narrow: 4 (over x, core).
Axes of the slice: x: 2, y: 2, z: 4, core: 2. Of those that a mesh axis runs over, the one named last changes fastest.
Arguments:
- logits: float32 [512, 32768], P(None, ('wide', 'narrow')), may hold values from -6 to 6
- filt: float32 [512], P(('wide', 'narrow')), may hold values from -6 to 6
- cells: float32 [512, 2048], P(('wide', 'narrow')), may hold values from 0.05 to 5
- cell_mask: int32 [512], replicated, may hold values 0 or 1
- gene_mask: int32 [8, 2048], replicated, may hold values 0 or 1
- slide_ids: int32 [32768], P(('wide', 'narrow')), may hold values from 0 to 7, never falling along the last dimension, each value on 1 to 8192 neighbouring positions
- target: float32 [32768, 2048], P(('wide', 'narrow')), may hold values from 0.05 to 5
- density: float32 [32768], P(('wide', 'narrow')), may hold values from 1 to 10
Outputs:
- loss_terms: float32 [3], replicated
- reg_terms: float32 [4], replicated
- g_pred: float32 [32768, 2048], P(('wide', 'narrow'))
- gene_cos: float32 [8, 2048], replicated
- spot_cos: float32 [32768], P(('wide', 'narrow'))
- grad_logits: float32 [512, 32768], P(None, ('wide', 'narrow'))
- grad_filter: float32 [512], P(('wide', 'narrow'))
- grad_cells: float32 [512, 2048], P(('wide', 'narrow'))
Inputs may be any that keep to these rules, and one draw needn't show every extreme that they name: `slide_ids`: each slide's spots form one run of consecutive positions, slides in increasing order, each with 1 to 8192 spots and one with exactly that many.
All inputs are finite; a program needn't handle non-finite values.
Results may differ from a plain program's by a relative error of at most 0.00015.
Values sent between devices are 32-bit elements; how exact they have to be, the bound alone decides.
A program may use at most 256 MiB of HBM per device.

v0:
```python
import jax
import jax.numpy as jnp
from jax import lax
from jax.experimental import pallas as pl
from jax.experimental.pallas import tpu as pltpu
from jax.sharding import PartitionSpec as P

eps = 1e-06
MESH = pl.DeviceIdType.MESH
bf16 = jnp.bfloat16
f32 = jnp.float32
LANES = 128
NCH = 8
TR = 256


def split(value):
    high = value.astype(bf16)
    return high, (value - high.astype(f32)).astype(bf16)


def mm(a, b):
    return lax.dot_general(a, b, (((1,), (0,)), ((), ())), preferred_element_type=f32)


def mm_nt(a, b):
    return lax.dot_general(a, b, (((1,), (1,)), ((), ())), preferred_element_type=f32)


def fused_kernel(
    logits_hbm, filt_ref, cells_hbm, mask_ref, gene_ref, ids_ref, target_hbm, dens_ref,
    terms_ref, reg_ref, pred_hbm, gcos_ref, scos_ref, glog_hbm, gfilt_ref, gcell_ref,
    lg, tv, pv, buf, chi, clo, fb, valid, keepc, whi, wlo, thi, tlo, gmb, oh, ohm, l1, l2,
    sd, sp, st, mass, rows, gph, gpl, gw, kp,
    stat, a1, a2, a3, gtot, gacc, kvec, k1, k2, k3,
    part, rb, sb, r1, tt_, r2, qq, r3,
    lsem, tsem, psem, osem,
    zs, zr, xs, xr, ys, yr, bs, br,
    fzs, fzr, fxs, fxr, fys, fyr, fbs, fbr,
    as1, ar1, as2, ar2, as3, ar3,
    ks1, kr1, ks2, kr2, ks3, kr3,
    cbs, cbr, cxs, cxr, cys, cyr, czs, czr,
):
    n_cells = chi.shape[1]
    width = chi.shape[2]
    spots = tv.shape[1]
    n_slides = gene_ref.shape[0]
    tiles = spots // LANES
    n_tiles = spots // TR
    wide, narrow = lax.axis_index("wide"), lax.axis_index("narrow")
    z, y = lax.div(wide, 2), lax.rem(wide, 2)
    x, core = lax.div(narrow, 2), lax.rem(narrow, 2)
    to_z = [(lax.rem(z + k, 4) * 2 + y, narrow) for k in (1, 2, 3)]
    from_z = [lax.rem(z + 4 - k, 4) for k in (1, 2, 3)]
    to_x = (wide, (1 - x) * 2 + core)
    to_y = (z * 2 + 1 - y, narrow)
    to_xy = (z * 2 + 1 - y, (1 - x) * 2 + core)
    to_b = (wide, x * 2 + 1 - core)

    def rcopy(src, dst, ss, rs, dev):
        return pltpu.make_async_remote_copy(
            src_ref=src, dst_ref=dst, send_sem=ss, recv_sem=rs, device_id=dev, device_id_type=MESH
        )

    def lanes(i, w=LANES):
        return pl.ds(pl.multiple_of(i * w, w), w)

    def own_cells(c, h):
        return pltpu.make_async_copy(
            cells_hbm.at[:, pl.ds((c * 2 + h) * LANES, LANES)], buf.at[c, h, z, y, x, core], lsem.at[c, h]
        )

    def get_logits(i):
        return pltpu.make_async_copy(logits_hbm.at[:, lanes(i)], lg.at[i], osem.at[i])

    def get_target(c):
        return pltpu.make_async_copy(target_hbm.at[:, lanes(c, width)], tv.at[c], tsem.at[c])

    def put_pred(c):
        return pltpu.make_async_copy(pv.at[c], pred_hbm.at[:, lanes(c, width)], psem.at[c])

    def put_glog(i):
        return pltpu.make_async_copy(gw.at[i], glog_hbm.at[:, lanes(i)], osem.at[i])

    for c in range(NCH):
        for h in range(2):
            own_cells(c, h).start()
    for i in range(tiles):
        get_logits(i).start()
    for c in range(NCH):
        get_target(c).start()

    barrier = pltpu.get_barrier_semaphore()
    for dev in to_z + [to_x, to_y, to_xy, to_b]:
        pl.semaphore_signal(barrier, inc=1, device_id=dev, device_id_type=MESH)

    row16 = lax.broadcasted_iota(jnp.int32, (16, LANES), 0)
    mine = jnp.zeros((16, LANES), f32)
    for r in range(16):
        mine = jnp.where(row16 == r, filt_ref[r], mine)
    fb[z, y, x, core] = mine
    for q in range(n_cells // LANES):
        line = mask_ref[q : q + 1, :].astype(f32)
        valid[q * LANES : (q + 1) * LANES, :] = jnp.broadcast_to(line, (LANES, LANES)).T
    pl.semaphore_wait(barrier, 7)

    def z_out(c, k):
        r = buf.at[c, :, z, y, x, core]
        return rcopy(r, r, zs.at[c, k], zr.at[c, k], to_z[k])

    def z_in(c, k):
        r = buf.at[c, :, from_z[k], y, x, core]
        return rcopy(r, r, zs.at[c, k], zr.at[c, k], to_z[k])

    def s1_out(c):
        a = buf.at[c, 0, :, y, x, core]
        b = buf.at[c, 1, :, y, x, core]
        return [rcopy(a, a, xs.at[c, 0], xr.at[c, 0], to_x), rcopy(b, b, ys.at[c, 0], yr.at[c, 0], to_y)]

    def s1_in(c):
        a = buf.at[c, 0, :, y, 1 - x, core]
        b = buf.at[c, 1, :, 1 - y, x, core]
        return [rcopy(a, a, xs.at[c, 0], xr.at[c, 0], to_x), rcopy(b, b, ys.at[c, 0], yr.at[c, 0], to_y)]

    def s2_out(c):
        a = buf.at[c, 0, :, y, :, core]
        b = buf.at[c, 1, :, :, x, core]
        return [rcopy(a, a, ys.at[c, 1], yr.at[c, 1], to_y), rcopy(b, b, xs.at[c, 1], xr.at[c, 1], to_x)]

    def s2_in(c):
        a = buf.at[c, 0, :, 1 - y, :, core]
        b = buf.at[c, 1, :, :, 1 - x, core]
        return [rcopy(a, a, ys.at[c, 1], yr.at[c, 1], to_y), rcopy(b, b, xs.at[c, 1], xr.at[c, 1], to_x)]

    def s3_out(c):
        r = buf.at[c, :, :, :, :, core]
        return rcopy(r, r, bs.at[c], br.at[c], to_b)

    def s3_in(c):
        r = buf.at[c, :, :, :, :, 1 - core]
        return rcopy(r, r, bs.at[c], br.at[c], to_b)

    def fz_out(k):
        r = fb.at[z, y, x, core]
        return rcopy(r, r, fzs.at[k], fzr.at[k], to_z[k])

    def fz_in(k):
        r = fb.at[from_z[k], y, x, core]
        return rcopy(r, r, fzs.at[k], fzr.at[k], to_z[k])

    def fx(at):
        r = fb.at[:, y, at, core]
        return rcopy(r, r, fxs.at[0], fxr.at[0], to_x)

    def fy(at):
        r = fb.at[:, at, :, core]
        return rcopy(r, r, fys.at[0], fyr.at[0], to_y)

    def fs(at):
        r = fb.at[:, :, :, at]
        return rcopy(r, r, fbs.at[0], fbr.at[0], to_b)

    def b1(c):
        return rcopy(stat.at[c], a1.at[c], as1.at[c], ar1.at[c], to_b)

    plane = [to_x, to_y, to_xy]
    here = y * 2 + x
    there = [y * 2 + 1 - x, (1 - y) * 2 + x, (1 - y) * 2 + 1 - x]

    def b2_out(c, k):
        r = a2.at[c, here]
        return rcopy(r, r, as2.at[c, k], ar2.at[c, k], plane[k])

    def b2_in(c, k):
        r = a2.at[c, there[k]]
        return rcopy(r, r, as2.at[c, k], ar2.at[c, k], plane[k])

    def b3_out(c, k):
        r = a3.at[c, z]
        return rcopy(r, r, as3.at[c, k], ar3.at[c, k], to_z[k])

    def b3_in(c, k):
        r = a3.at[c, from_z[k]]
        return rcopy(r, r, as3.at[c, k], ar3.at[c, k], to_z[k])

    def sum_second(c):
        b1(c).wait_recv()
        a2[c, here] = stat[c] + a1[c]
        for k in range(3):
            b2_out(c, k).start()

    def sum_third(c):
        for k in range(3):
            b2_in(c, k).wait_recv()
        a3[c, z] = (a2[c, 0] + a2[c, 1]) + (a2[c, 2] + a2[c, 3])
        for k in range(3):
            b3_out(c, k).start()

    def sum_last(c):
        for k in range(3):
            b3_in(c, k).wait_recv()
        return (a3[c, 0] + a3[c, 1]) + (a3[c, 2] + a3[c, 3])

    def softmax(i, ent):
        get_logits(i).wait()
        value = lg[i]
        top = jnp.max(value, axis=0, keepdims=True)
        expo = jnp.exp(value - top) * valid[...]
        total = jnp.sum(expo, axis=0, keepdims=True)
        prob = expo * (1.0 / total)
        lg[i] = prob
        return ent + jnp.sum(prob * (value - top - jnp.log(total)), axis=0, keepdims=True)

    def one_hot(i, _):
        ids = ids_ref[pl.ds(i, 1), :]
        square = (lax.broadcasted_iota(jnp.int32, (LANES, LANES), 0) == ids).astype(f32)
        oh[lanes(i), :] = square.T.astype(bf16)
        ohm[:, lanes(i)] = square[:16, :].astype(bf16)
        return 0

    def weights(i, _):
        w = lg[i] * keepc[...]
        mass[pl.ds(i, 1), :] = jnp.sum(w, axis=0, keepdims=True)
        high, low = split(w)
        whi[:, lanes(i)] = high
        wlo[:, lanes(i)] = low
        turned = w.T
        high, low = split(turned)
        thi[lanes(i), :] = high
        tlo[lanes(i), :] = low
        return 0

    for k in range(3):
        fz_out(k).start()
    for c in range(NCH):
        for h in range(2):
            own_cells(c, h).wait()
        for k in range(3):
            z_out(c, k).start()

    def gather_tick(t):
        def stage_one(c):
            for k in range(3):
                z_in(c, k).wait_recv()
            for d in s1_out(c):
                d.start()

        def stage_two(c):
            for d in s1_in(c):
                d.wait_recv()
            for d in s2_out(c):
                d.start()

        def stage_three(c):
            for d in s2_in(c):
                d.wait_recv()
            s3_out(c).start()

        for lag, stage in ((0, stage_one), (1, stage_two), (2, stage_three)):
            if isinstance(t, int):
                if 0 <= t - lag < NCH:
                    stage(t - lag)
            else:
                pl.when(jnp.logical_and(t - lag >= 0, t - lag < NCH))(lambda s=stage, c=t - lag: s(c))

    for k in range(3):
        fz_in(k).wait_recv()
    fx(x).start()
    gather_tick(0)
    for c in range(NCH):
        gm = jnp.concatenate(
            [gene_ref[:, c * width : (c + 1) * width].astype(f32), jnp.zeros((LANES - n_slides, width), f32)], axis=0
        )
        gmb[c] = gm.astype(bf16)
    ent = lax.fori_loop(0, tiles // 2, softmax, jnp.zeros((1, LANES), f32))
    fx(1 - x).wait_recv()
    fy(y).start()
    gather_tick(1)
    ent = lax.fori_loop(tiles // 2, tiles, softmax, ent)
    fy(1 - y).wait_recv()
    fs(core).start()
    gather_tick(2)
    lax.fori_loop(0, tiles, one_hot, 0)
    fs(1 - core).wait_recv()
    keepc[...] = jax.nn.sigmoid(fb[...].reshape(n_cells, LANES))
    lax.fori_loop(0, tiles, weights, 0)
    sd[...] = jnp.zeros_like(sd)
    sp[...] = jnp.zeros_like(sp)
    st[...] = jnp.zeros_like(st)

    def fold(v):
        out = v[:, :LANES]
        for k in range(1, v.shape[1] // LANES):
            out = out + v[:, k * LANES : (k + 1) * LANES]
        return out

    def forward(c):
        s3_in(c).wait_recv()
        get_target(c).wait()
        whole = jnp.concatenate([buf[c, h].reshape(n_cells, LANES) for h in range(2)], axis=1)
        high, low = split(whole)
        chi[c] = high
        clo[c] = low

        def rows_of(r, sums):
            at = pl.ds(pl.multiple_of(r * TR, TR), TR)
            wh, wl = thi[at, :], tlo[at, :]
            ch, cl = chi[c], clo[c]
            pred = mm(jnp.concatenate([wh, wl, wh], axis=1), jnp.concatenate([ch, ch, cl], axis=0))
            pv[c, at, :] = pred
            tgt = tv[c, at, :]
            seen = mm(oh[at, :], gmb[c])
            who = ohm[:, at]
            who = jnp.concatenate([who, who], axis=1)
            out = []
            for prod, spot in ((pred * tgt, sd), (pred * pred, sp), (tgt * tgt, st)):
                spot[at, :] += fold(seen * prod)
                ph, plo = split(prod)
                out.append(mm(who, jnp.concatenate([ph, plo], axis=0)))
            return tuple(a + b for a, b in zip(sums, out))

        zero = jnp.zeros((16, width), f32)
        sums = lax.fori_loop(0, n_tiles, rows_of, (zero, zero, zero))
        for k in range(3):
            stat[c, k * 8 : (k + 1) * 8, :] = sums[k][:8, :]
        put_pred(c).start()

    zero8 = jnp.zeros((8, width), f32)

    def middle(t, _):
        gather_tick(t)
        c = t - 3
        forward(c)
        stat[c, 24:32, :] = zero8
        b1(c).start()
        pl.when(c >= 1)(lambda: sum_second(c - 1))
        pl.when(c >= 2)(lambda: sum_third(c - 2))
        return 0

    lax.fori_loop(3, NCH + 2, middle, 0)
    last = NCH - 1
    forward(last)

    def spot_rows(i, _):
        for k, ref in enumerate((sd, sp, st)):
            rows[k, pl.ds(i, 1), :] = jnp.sum(ref[lanes(i), :].T, axis=0, keepdims=True)
        return 0

    lax.fori_loop(0, tiles, spot_rows, 0)
    sdot, spp, stt = rows[0], rows[1], rows[2]
    scale = lax.rsqrt(spp + eps) * lax.rsqrt(stt + eps)
    scos = sdot * scale
    scos_ref[...] = scos
    shrink = scale * (sdot / (spp + eps))
    for k, value in ((0, scale), (1, shrink)):
        high, low = split(value)
        rows[2 * k] = high.astype(f32)
        rows[2 * k + 1] = low.astype(f32)
    dens = dens_ref[...]
    mass_row = mass[...]
    rows[4] = dens * (jnp.log(dens) - jnp.log(mass_row))

    iota8 = lax.broadcasted_iota(jnp.int32, (8, LANES), 0)
    lane8 = lax.broadcasted_iota(jnp.int32, (8, LANES), 1)

    def coef_rows(i, sums):
        mine = (iota8 == ids_ref[pl.ds(i, 1), :]).astype(f32)
        pad = jnp.zeros((LANES - 32, LANES), f32)
        at = pl.ds(i, 1)
        for k, ref in ((0, l1), (1, l2)):
            ref[lanes(i), :] = jnp.concatenate(
                [mine, mine, mine * rows[2 * k, at, :], mine * rows[2 * k + 1, at, :], pad], axis=0
            ).T.astype(bf16)
        return (
            sums[0] + mine * mass[at, :],
            sums[1] + mine * dens_ref[at, :],
            sums[2] + mine * rows[4, at, :],
        )

    zero = jnp.zeros((8, LANES), f32)
    totals = lax.fori_loop(0, tiles, coef_rows, (zero, zero, zero))
    extra = zero
    for k, value in enumerate(totals):
        extra = jnp.where(lane8 == k, jnp.sum(value, axis=1, keepdims=True), extra)
    extra = jnp.where(jnp.logical_and(lane8 == 3, iota8 == 0), -jnp.sum(scos), extra)
    extra = jnp.where(jnp.logical_and(lane8 == 4, iota8 == 0), -jnp.sum(ent), extra)
    stat[last, 24:32, :] = jnp.concatenate([extra] + [zero] * (width // LANES - 1), axis=1)
    b1(last).start()
    sum_second(last - 1)
    sum_third(last - 2)

    gacc[...] = jnp.zeros_like(gacc)
    gw[...] = jnp.zeros_like(gw)

    def scatter_sib(c):
        return rcopy(part.at[c, :, :, :, :, 1 - core], rb.at[c], cbs.at[c], cbr.at[c], to_b)

    def scatter_one(c):
        return [
            rcopy(sb.at[c, 0, :, 1 - y], r1.at[c, 0], cys.at[c, 0], cyr.at[c, 0], to_y),
            rcopy(sb.at[c, 1, :, :, 1 - x], r1.at[c, 1], cxs.at[c, 0], cxr.at[c, 0], to_x),
        ]

    def scatter_two(c):
        return [
            rcopy(tt_.at[c, 0, :, 1 - x], r2.at[c, 0], cxs.at[c, 1], cxr.at[c, 1], to_x),
            rcopy(tt_.at[c, 1, :, 1 - y], r2.at[c, 1], cys.at[c, 1], cyr.at[c, 1], to_y),
        ]

    def scatter_z(c, k):
        return rcopy(qq.at[c, :, lax.rem(z + k + 1, 4)], r3.at[c, k], czs.at[c, k], czr.at[c, k], to_z[k])

    def sc1(c):
        scatter_sib(c).wait_recv()
        sb[c] = part[c, :, :, :, :, core] + rb[c]
        for d in scatter_one(c):
            d.start()

    def sc2(c):
        for d in scatter_one(c):
            d.wait_recv()
        tt_[c, 0] = sb[c, 0, :, y] + r1[c, 0]
        tt_[c, 1] = sb[c, 1, :, :, x] + r1[c, 1]
        for d in scatter_two(c):
            d.start()

    def sc3(c):
        for d in scatter_two(c):
            d.wait_recv()
        qq[c, 0] = tt_[c, 0, :, x] + r2[c, 0]
        qq[c, 1] = tt_[c, 1, :, y] + r2[c, 1]
        for k in range(3):
            scatter_z(c, k).start()

    def sc4(c):
        for k in range(3):
            scatter_z(c, k).wait_recv()
        for h in range(2):
            gcell_ref[:, lanes(c * 2 + h)] = (qq[c, h, z] + r3[c, 0, h]) + (r3[c, 1, h] + r3[c, 2, h])

    def backward(c):
        total = sum_last(c)
        gtot[c] = total
        dot_s, pp_s, tt_s = total[0:8], total[8:16], total[16:24]
        gm = gene_ref[:, lanes(c, width)].astype(f32)
        gscale = gm * lax.rsqrt(pp_s + eps) * lax.rsqrt(tt_s + eps)
        gcos = dot_s * gscale
        gcos_ref[:, lanes(c, width)] = gcos
        gacc[...] += gcos
        gshrink = gscale * (dot_s / (pp_s + eps))
        pad = jnp.zeros((LANES - 32, width), f32)
        coefs = []
        for value in (gscale, gshrink):
            high, low = split(value)
            coefs.append(
                jnp.concatenate([high.astype(f32), low.astype(f32), gm, gm, pad], axis=0).astype(bf16)
            )

        def rows_of(r, _):
            at = pl.ds(pl.multiple_of(r * TR, TR), TR)
            grad = mm(l2[at, :], coefs[1]) * pv[c, at, :] - mm(l1[at, :], coefs[0]) * tv[c, at, :]
            high, low = split(grad)
            gph[at, :] = high
            gpl[at, :] = low
            return 0

        lax.fori_loop(0, n_tiles, rows_of, 0)

        def cells_of(r, _):
            at = pl.ds(pl.multiple_of(r * LANES, LANES), LANES)
            wh, wl = whi[at, :], wlo[at, :]
            gh, gl = gph[...], gpl[...]
            out = mm(jnp.concatenate([wh, wl, wh], axis=1), jnp.concatenate([gh, gh, gl], axis=0))
            for h in range(2):
                part[c, h, r] = out[:, h * LANES : (h + 1) * LANES].reshape(2, 2, 2, 16, LANES)
            return 0

        lax.fori_loop(0, n_cells // LANES, cells_of, 0)
        scatter_sib(c).start()

        def spots_of(r, _):
            at = pl.ds(pl.multiple_of(r * TR, TR), TR)
            ch, cl = chi[c], clo[c]
            gh, gl = gph[at, :], gpl[at, :]
            out = mm_nt(jnp.concatenate([ch, cl, ch], axis=1), jnp.concatenate([gh, gh, gl], axis=1))
            for h in range(TR // LANES):
                gw[r * (TR // LANES) + h] += out[:, h * LANES : (h + 1) * LANES]
            return 0

        lax.fori_loop(0, n_tiles, spots_of, 0)

    def back_tick(t, _):
        backward(t)
        pl.when(t == 0)(lambda: sum_second(last))
        pl.when(t == 0)(lambda: sum_third(last - 1))
        pl.when(t == 1)(lambda: sum_third(last))
        pl.when(t >= 1)(lambda: sc1(t - 1))
        pl.when(t >= 2)(lambda: sc2(t - 2))
        pl.when(t >= 3)(lambda: sc3(t - 3))
        pl.when(t >= 4)(lambda: sc4(t - 4))
        return 0

    lax.fori_loop(0, NCH, back_tick, 0)
    sc1(last)
    sc2(last - 1)
    sc3(last - 2)

    sums_s = gtot[last, 24:32, :LANES]
    mass_s, wsum_s, logsum_s = sums_s[:, 0:1], sums_s[:, 1:2], sums_s[:, 2:3]
    kp[...] = jnp.zeros_like(kp)

    def finish(i, _):
        at = pl.ds(i, 1)
        mine = (iota8 == ids_ref[at, :]).astype(f32)
        mass_at = jnp.sum(mine * mass_s, axis=0, keepdims=True)
        wsum_at = jnp.sum(mine * wsum_s, axis=0, keepdims=True)
        gmass = -(dens_ref[at, :] / wsum_at) / mass[at, :] + 1.0 / mass_at
        prob = lg[i]
        grad = gw[i] + gmass
        kp[...] += prob * grad
        grad = keepc[...] * grad
        middle_ = jnp.sum(prob * grad, axis=0, keepdims=True)
        gw[i] = prob * (grad - middle_)
        put_glog(i).start()
        return 0

    lax.fori_loop(0, tiles, finish, 0)
    quarter = n_cells // LANES
    rows_k, rows_keep = [], []
    for q in range(quarter):
        rows_k.append(jnp.sum(kp[q * LANES : (q + 1) * LANES, :].T, axis=0, keepdims=True))
        rows_keep.append(keepc[q * LANES : (q + 1) * LANES, :].T[0:1, :])
    blank = jnp.zeros((8 - quarter, LANES), f32)
    kvec[...] = jnp.concatenate(rows_k + [blank], axis=0)
    keep = jnp.concatenate(rows_keep, axis=0)

    k1_copy = rcopy(kvec, k1, ks1.at[0], kr1.at[0], to_b)

    def k2_copy(slot, k):
        return rcopy(k2.at[slot], k2.at[slot], ks2.at[k], kr2.at[k], plane[k])

    def k3_copy(slot, k):
        return rcopy(k3.at[slot], k3.at[slot], ks3.at[k], kr3.at[k], to_z[k])

    k1_copy.start()
    sc2(last)
    sc3(last - 1)
    sc4(last - 3)
    k1_copy.wait_recv()
    k2[here] = kvec[...] + k1[...]
    for k in range(3):
        k2_copy(here, k).start()
    sc3(last)
    sc4(last - 2)
    for k in range(3):
        k2_copy(there[k], k).wait_recv()
    k3[z] = (k2[0] + k2[1]) + (k2[2] + k2[3])
    for k in range(3):
        k3_copy(z, k).start()

    ok = mask_ref[...].astype(f32)
    count = jnp.sum(ok * keep)
    target_count = n_cells // 4
    count_term = jnp.abs(count - target_count) / n_cells
    binarity = jnp.sum(ok * (keep - keep * keep)) / n_cells
    gene_loss = -jnp.sum(gacc[...])
    spot_loss = jnp.sum(jnp.where(jnp.logical_and(lane8 == 3, iota8 == 0), sums_s, 0.0))
    entropy = jnp.sum(jnp.where(jnp.logical_and(lane8 == 4, iota8 == 0), sums_s, 0.0)) / (spots * 32)
    kl = jnp.sum(logsum_s / wsum_s + jnp.log(mass_s) - jnp.log(wsum_s))
    terms_ref[0] = gene_loss + spot_loss + kl + count_term + binarity
    terms_ref[1] = gene_loss
    terms_ref[2] = spot_loss
    reg_ref[0] = kl
    reg_ref[1] = count_term
    reg_ref[2] = binarity
    reg_ref[3] = entropy

    sc4(last - 1)
    for k in range(3):
        k3_copy(from_z[k], k).wait_recv()
    total = ((k3[0] + k3[1]) + (k3[2] + k3[3]))[:quarter, :]
    off = count - target_count
    sign = jnp.where(off > 0, 1.0, jnp.where(off < 0, -1.0, 0.0))
    total = total + ok * (sign + 1.0 - 2.0 * keep) / n_cells
    total = total * keep * (1.0 - keep)
    kvec_out = jnp.concatenate([total, blank], axis=0)
    dev = wide * 4 + narrow
    picked = jnp.sum(jnp.where(iota8 == lax.div(dev, 8), kvec_out, 0.0), axis=0, keepdims=True)
    picked = pltpu.roll(picked, lax.rem(LANES - lax.rem(dev, 8) * 16, LANES), 1)
    gfilt_ref[...] = picked[:, :16]
    sc4(last)

    def leave(c, _):
        for k in range(3):
            z_out(c, k).wait_send()
            b2_out(c, k).wait_send()
            b3_out(c, k).wait_send()
            scatter_z(c, k).wait_send()
        for d in s1_out(c) + s2_out(c) + scatter_one(c) + scatter_two(c):
            d.wait_send()
        s3_out(c).wait_send()
        b1(c).wait_send()
        scatter_sib(c).wait_send()
        put_pred(c).wait()
        return 0

    lax.fori_loop(0, NCH, leave, 0)
    for i in range(tiles):
        put_glog(i).wait()
    for k in range(3):
        fz_out(k).wait_send()
        k2_copy(here, k).wait_send()
        k3_copy(z, k).wait_send()
    fx(x).wait_send()
    fy(y).wait_send()
    fs(core).wait_send()
    k1_copy.wait_send()


def fused(logits, filt, cells, cell_mask, gene_mask, slide_ids, target, density):
    n_cells, spots = logits.shape
    own, genes = cells.shape
    n_slides = gene_mask.shape[0]
    width = genes // NCH
    tiles = spots // LANES
    dma = pltpu.SemaphoreType.DMA
    vmem, anywhere = pltpu.VMEM, pl.BlockSpec(memory_space=pl.ANY)
    inside = pl.BlockSpec(memory_space=pltpu.VMEM)
    scalars = pl.BlockSpec(memory_space=pltpu.SMEM)
    ring = (4, 2, 2, 2, 16, LANES)
    scratch = [
        vmem((tiles, n_cells, LANES), f32),
        vmem((NCH, spots, width), f32),
        vmem((NCH, spots, width), f32),
        vmem((NCH, 2) + ring, f32),
        vmem((NCH, n_cells, width), bf16),
        vmem((NCH, n_cells, width), bf16),
        vmem(ring, f32),
        vmem((n_cells, LANES), f32),
        vmem((n_cells, LANES), f32),
        vmem((n_cells, spots), bf16),
        vmem((n_cells, spots), bf16),
        vmem((spots, n_cells), bf16),
        vmem((spots, n_cells), bf16),
        vmem((NCH, LANES, width), bf16),
        vmem((spots, LANES), bf16),
        vmem((16, spots), bf16),
        vmem((spots, LANES), bf16),
        vmem((spots, LANES), bf16),
        vmem((spots, LANES), f32),
        vmem((spots, LANES), f32),
        vmem((spots, LANES), f32),
        vmem((8, LANES), f32),
        vmem((5, 8, LANES), f32),
        vmem((spots, width), bf16),
        vmem((spots, width), bf16),
        vmem((tiles, n_cells, LANES), f32),
        vmem((n_cells, LANES), f32),
        vmem((NCH, 32, width), f32),
        vmem((NCH, 32, width), f32),
        vmem((NCH, 4, 32, width), f32),
        vmem((NCH, 4, 32, width), f32),
        vmem((NCH, 32, width), f32),
        vmem((8, width), f32),
        vmem((8, LANES), f32),
        vmem((8, LANES), f32),
        vmem((4, 8, LANES), f32),
        vmem((4, 8, LANES), f32),
        vmem((NCH, 2) + ring, f32),
        vmem((NCH, 2, 4, 2, 2, 16, LANES), f32),
        vmem((NCH, 2, 4, 2, 2, 16, LANES), f32),
        vmem((NCH, 2, 4, 2, 16, LANES), f32),
        vmem((NCH, 2, 4, 2, 16, LANES), f32),
        vmem((NCH, 2, 4, 16, LANES), f32),
        vmem((NCH, 2, 4, 16, LANES), f32),
        vmem((NCH, 3, 2, 16, LANES), f32),
        dma((NCH, 2)), dma((NCH,)), dma((NCH,)), dma((tiles,)),
        dma((NCH, 3)), dma((NCH, 3)), dma((NCH, 2)), dma((NCH, 2)), dma((NCH, 2)), dma((NCH, 2)), dma((NCH,)), dma((NCH,)),
        dma((3,)), dma((3,)), dma((1,)), dma((1,)), dma((1,)), dma((1,)), dma((1,)), dma((1,)),
        dma((NCH,)), dma((NCH,)), dma((NCH, 3)), dma((NCH, 3)), dma((NCH, 3)), dma((NCH, 3)),
        dma((1,)), dma((1,)), dma((3,)), dma((3,)), dma((3,)), dma((3,)),
        dma((NCH,)), dma((NCH,)), dma((NCH, 2)), dma((NCH, 2)), dma((NCH, 2)), dma((NCH, 2)), dma((NCH, 3)), dma((NCH, 3)),
    ]
    out = pl.pallas_call(
        fused_kernel,
        out_shape=(
            jax.ShapeDtypeStruct((3,), f32),
            jax.ShapeDtypeStruct((4,), f32),
            jax.ShapeDtypeStruct((spots, genes), f32),
            jax.ShapeDtypeStruct((n_slides, genes), f32),
            jax.ShapeDtypeStruct((tiles, LANES), f32),
            jax.ShapeDtypeStruct((n_cells, spots), f32),
            jax.ShapeDtypeStruct((1, own), f32),
            jax.ShapeDtypeStruct((own, genes), f32),
        ),
        in_specs=[anywhere, scalars, anywhere, inside, inside, inside, anywhere, inside],
        out_specs=(scalars, scalars, anywhere, inside, inside, anywhere, inside, inside),
        scratch_shapes=scratch,
        compiler_params=pltpu.CompilerParams(
            collective_id=0, has_side_effects=True, vmem_limit_bytes=60 << 20
        ),
    )(
        logits, filt, cells, cell_mask.reshape(n_cells // LANES, LANES), gene_mask,
        slide_ids.reshape(tiles, LANES), target, density.reshape(tiles, LANES),
    )
    terms, reg, pred, gcos, scos, glog, gfilt, gcell = out
    return terms, reg, pred, gcos, scos.reshape(spots), glog, gfilt.reshape(own), gcell


def per_slide(onehot, values):
    return lax.dot_general(
        onehot, values, (((0,), (0,)), ((), ())), precision=lax.Precision.HIGHEST
    )


def on_device(logits, filt, cells, cell_mask, gene_mask, slide_ids, target, density):
    high = lax.Precision.HIGHEST
    n_cells = logits.shape[0]
    own_rows = cells.shape[0]
    n_slides = gene_mask.shape[0]
    valid = cell_mask.astype(jnp.float32)
    top = jnp.max(logits, axis=0, keepdims=True)
    expo = jnp.exp(logits - top) * valid[:, None]
    total = jnp.sum(expo, axis=0, keepdims=True)
    prob = expo / total
    logp = jnp.where(valid[:, None] > 0, logits - top - jnp.log(total), 0.0)
    entropy_part = -jnp.sum(prob * logp)
    whole, filt_all = (
        lax.all_gather(cells, ("wide", "narrow"), axis=0, tiled=True),
        lax.all_gather(filt, ("wide", "narrow"), axis=0, tiled=True),
    )
    keep = jax.nn.sigmoid(filt_all)
    weighted = prob * keep[:, None]
    g_pred = lax.dot_general(weighted, whole, (((0,), (0,)), ((), ())), precision=high)
    onehot = (slide_ids[:, None] == jnp.arange(n_slides, dtype=jnp.int32)[None, :]).astype(
        jnp.float32
    )
    gmask = gene_mask.astype(jnp.float32)
    spot_mask = jnp.dot(onehot, gmask, precision=high)
    masked_pred = spot_mask * g_pred
    sdot = jnp.sum(masked_pred * target, axis=1)
    spp = jnp.sum(masked_pred * g_pred, axis=1)
    stt = jnp.sum(spot_mask * target * target, axis=1)
    spot_scale = lax.rsqrt(spp + eps) * lax.rsqrt(stt + eps)
    spot_cos = sdot * spot_scale
    mass = jnp.sum(weighted, axis=0)
    log_part = density * (jnp.log(density) - jnp.log(mass))
    slide_vec = jnp.stack([mass, density, log_part], axis=1)
    loss_parts = jnp.stack([-jnp.sum(spot_cos), entropy_part])
    dot_s, pp_s, tt_s, slide_tot, loss_tot = lax.psum(
        (
            per_slide(onehot, g_pred * target),
            per_slide(onehot, g_pred * g_pred),
            per_slide(onehot, target * target),
            per_slide(onehot, slide_vec),
            loss_parts,
        ),
        ("wide", "narrow"),
    )
    mass_s = slide_tot[:, 0]
    wsum_s = slide_tot[:, 1]
    logsum_s = slide_tot[:, 2]
    gene_scale = gmask * lax.rsqrt(pp_s + eps) * lax.rsqrt(tt_s + eps)
    gene_cos = dot_s * gene_scale
    gene_loss = -jnp.sum(gene_cos)
    spot_loss = loss_tot[0]
    entropy = loss_tot[1] / (prob.shape[1] * lax.axis_size(("wide", "narrow")))
    kl_term = jnp.sum(logsum_s / wsum_s) + jnp.sum(jnp.log(mass_s) - jnp.log(wsum_s))
    count = jnp.sum(valid * keep)
    target_count = n_cells // 4
    count_term = jnp.abs(count - target_count) / n_cells
    binarity = jnp.sum(valid * (keep - keep * keep)) / n_cells
    loss = gene_loss + spot_loss + kl_term + count_term + binarity
    terms = jnp.stack([loss, gene_loss, spot_loss])
    reg_terms = jnp.stack([kl_term, count_term, binarity, entropy])
    gene_shrink = gene_scale * dot_s / (pp_s + eps)
    grad_pred = -jnp.dot(onehot, gene_scale, precision=high) * target
    grad_pred = grad_pred + jnp.dot(onehot, gene_shrink, precision=high) * g_pred
    spot_shrink = sdot / (spp + eps)
    grad_pred = grad_pred - spot_mask * spot_scale[:, None] * (
        target - spot_shrink[:, None] * g_pred
    )
    spot_slide = jnp.dot(onehot, jnp.stack([mass_s, wsum_s], axis=1), precision=high)
    grad_mass = -(density / spot_slide[:, 1]) / mass + 1.0 / spot_slide[:, 0]
    grad_weighted = lax.dot_general(whole, grad_pred, (((1,), (1,)), ((), ())), precision=high)
    grad_weighted = grad_weighted + grad_mass[None, :]
    grad_prob = keep[:, None] * grad_weighted
    keep_part = jnp.sum(prob * grad_weighted, axis=1)
    grad_logits = prob * (grad_prob - jnp.sum(prob * grad_prob, axis=0, keepdims=True))
    cell_part = jnp.dot(weighted, grad_pred, precision=high)
    grad_cells, keep_sum = (
        lax.psum_scatter(cell_part, ("wide", "narrow"), scatter_dimension=0, tiled=True),
        lax.psum_scatter(keep_part, ("wide", "narrow"), scatter_dimension=0, tiled=True),
    )
    first_row = lax.axis_index(("wide", "narrow")) * own_rows
    own_keep = lax.dynamic_slice_in_dim(keep, first_row, own_rows, 0)
    own_valid = lax.dynamic_slice_in_dim(valid, first_row, own_rows, 0)
    keep_grad = (
        keep_sum + own_valid * (jnp.sign(count - target_count) + 1.0 - 2.0 * own_keep) / n_cells
    )
    grad_filter = keep_grad * own_keep * (1.0 - own_keep)
    return (terms, reg_terms, g_pred, gene_cos, spot_cos, grad_logits, grad_filter, grad_cells)


def fits_fused(mesh, logits, cells, gene_mask, slide_ids):
    n_cells, spots = logits.shape
    return (
        (mesh.shape["wide"], mesh.shape["narrow"]) == (8, 4)
        and cells.shape == (16, 2048)
        and n_cells == 512
        and spots == 1024
        and gene_mask.shape[0] == 8
    )


def solution(mesh):
    def step(logits, filt, cells, cell_mask, gene_mask, slide_ids, target, density):
        fits = fits_fused(mesh, logits, cells, gene_mask, slide_ids)
        run = fused if fits else on_device
        return run(logits, filt, cells, cell_mask, gene_mask, slide_ids, target, density)

    placed = (
        P(None, ("wide", "narrow")),
        P(("wide", "narrow")),
        P(("wide", "narrow"), None),
        P(),
        P(),
        P(("wide", "narrow")),
        P(("wide", "narrow"), None),
        P(("wide", "narrow")),
    )
    return jax.shard_map(
        step,
        mesh=mesh,
        in_specs=placed,
        out_specs=(
            P(),
            P(),
            P(("wide", "narrow"), None),
            P(),
            P(("wide", "narrow")),
            P(None, ("wide", "narrow")),
            P(("wide", "narrow")),
            P(("wide", "narrow"), None),
        ),
        check_vma=False,
    )
```

profile of v0, /device:TPU:0, one launch (start us, length us, event | category | flops | bytes accessed | tf_op | source)
XLA Modules:
  0.0 120.1 jit_solution(2502563931135865786)
XLA Ops:
  0.6 105.4 %shard_map.143 = (f32[3]{0:T(128)}, f32[4]{0:T(128)}, f32[1024,2048]{1,0:T(8,128)}, f32[8,2048]{1,0:T(8,128)}, f32[8,128]{1,0:T(8,128)}, /*index=5*/f32[512,1024...) custom-call(f32[512,1024]{1,0:T(8,128)} %logits_hbm.1, f32[16]{0:T(128)} %filt_ref.1, f32[16,2048]{1,0:T(8,128)} %cells_hbm.1, ...), custom_call_target="tpu_custom_call" | custom-call | tf_op jit(solution)/shard_map/pallas_call | solution.py:684
  106.1 1.2 copy.24
  107.2 1.1 copy.25
  108.3 0.0 copy-start.2
  108.3 0.0 copy-start.3
  108.3 0.0 copy-start
  108.3 0.0 copy-start.4
  108.3 0.0 copy-start.1
  108.4 8.0 %copy.26 = f32[1024,2048]{1,0:T(8,128)} copy(f32[1024,2048]{1,0:T(8,128)} %get-tuple-element.34) | data formatting | bytes 16777216
  116.4 0.0 copy-done.2
  116.4 0.6 copy.27
  117.0 0.0 copy-done.3
  117.0 0.6 copy.28
  117.6 0.0 copy-done
  117.6 1.3 %copy.29 = f32[512,1024]{1,0:T(8,128)} copy(f32[512,1024]{1,0:T(8,128)S(1)} %copy-done) | data formatting | bytes 4194304
  119.0 0.0 copy-done.4
  119.0 0.5 copy.30
  119.5 0.0 copy-done.1
  119.5 0.7 copy.31
Async XLA Ops:
  108.3 8.1 %copy-start.2 = (f32[8,2048]{1,0:T(8,128)S(1)}, f32[8,2048]{1,0:T(8,128)}, u32[]{:S(2)}) copy-start(f32[8,2048]{1,0:T(8,128)} %get-tuple-element.35) | copy-start | bytes 196612
  108.3 8.7 %copy-start.3 = (f32[8,128]{1,0:T(8,128)S(1)}, f32[8,128]{1,0:T(8,128)}, u32[]{:S(2)}) copy-start(f32[8,128]{1,0:T(8,128)} %get-tuple-element.20) | copy-start | bytes 12292
  108.3 9.3 %copy-start = (f32[512,1024]{1,0:T(8,128)S(1)}, f32[512,1024]{1,0:T(8,128)}, u32[]{:S(2)}) copy-start(f32[512,1024]{1,0:T(8,128)} %get-tuple-element.37) | copy-start | bytes 6291460
  108.3 10.6 %copy-start.4 = (f32[1,16]{1,0:T(1,128)S(1)}, f32[1,16]{1,0:T(1,128)}, u32[]{:S(2)}) copy-start(f32[1,16]{1,0:T(1,128)} %get-tuple-element.22) | copy-start | bytes 196
  108.3 11.1 %copy-start.1 = (f32[16,2048]{1,0:T(8,128)S(1)}, f32[16,2048]{1,0:T(8,128)}, u32[]{:S(2)}) copy-start(f32[16,2048]{1,0:T(8,128)} %get-tuple-element.39) | copy-start | bytes 393220
where the time goes:
time: 120 us
  Pallas kernels  105 us (88%)
  local copies, waits for them, and re-layouts  14 us (12%)
    pallas_call x1, Pallas kernels, fused(): pl.pallas_call(fused_kernel, out_shape=(jax.ShapeDtypeStruct((3,), f32),...  105 us
    unnamed x18, local copies, waits for them, and re-layouts  14 us

commit v1 on v0

--- a/solution.py
+++ b/solution.py
@@ -11,7 +11,8 @@
 f32 = jnp.float32
 LANES = 128
 NCH = 8
-TR = 256
+BR = 32
+HELD = 4
 
 
 def split(value):
@@ -29,24 +30,24 @@
 
 def fused_kernel(
     logits_hbm, filt_ref, cells_hbm, mask_ref, gene_ref, ids_ref, target_hbm, dens_ref,
-    terms_ref, reg_ref, pred_hbm, gcos_ref, scos_ref, glog_hbm, gfilt_ref, gcell_ref,
-    lg, tv, pv, buf, chi, clo, fb, valid, keepc, whi, wlo, thi, tlo, gmb, oh, ohm, l1, l2,
-    sd, sp, st, mass, rows, gph, gpl, gw, kp,
-    stat, a1, a2, a3, gtot, gacc, kvec, k1, k2, k3,
+    pv, lg, gw, keepc, gmass_ref, gacc, sums_ref, keep_ref, gcos_ref, scos_ref, gfilt_ref, gcell_ref,
+    tv, buf, chi, clo, fb, valid, whi, wlo, thi, tlo, gmb, oh, l1, l2,
+    idc, seen, blocks, sd, sp, st, mass, rows, gph, gpl, kp,
+    stat, a1, a2, a3, fin, kvec, k1, k2, k3,
     part, rb, sb, r1, tt_, r2, qq, r3,
-    lsem, tsem, psem, osem,
+    lsem, tsem, osem,
     zs, zr, xs, xr, ys, yr, bs, br,
     fzs, fzr, fxs, fxr, fys, fyr, fbs, fbr,
-    as1, ar1, as2, ar2, as3, ar3,
+    as1, ar1, as2, ar2, as3, ar3, as4, ar4,
     ks1, kr1, ks2, kr2, ks3, kr3,
     cbs, cbr, cxs, cxr, cys, cyr, czs, czr,
 ):
     n_cells = chi.shape[1]
     width = chi.shape[2]
-    spots = tv.shape[1]
+    n_blocks = tv.shape[1]
+    spots = n_blocks * BR
     n_slides = gene_ref.shape[0]
     tiles = spots // LANES
-    n_tiles = spots // TR
     wide, narrow = lax.axis_index("wide"), lax.axis_index("narrow")
     z, y = lax.div(wide, 2), lax.rem(wide, 2)
     x, core = lax.div(narrow, 2), lax.rem(narrow, 2)
@@ -74,13 +75,7 @@
         return pltpu.make_async_copy(logits_hbm.at[:, lanes(i)], lg.at[i], osem.at[i])
 
     def get_target(c):
-        return pltpu.make_async_copy(target_hbm.at[:, lanes(c, width)], tv.at[c], tsem.at[c])
-
-    def put_pred(c):
-        return pltpu.make_async_copy(pv.at[c], pred_hbm.at[:, lanes(c, width)], psem.at[c])
-
-    def put_glog(i):
-        return pltpu.make_async_copy(gw.at[i], glog_hbm.at[:, lanes(i)], osem.at[i])
+        return pltpu.make_async_copy(target_hbm.at[:, :, lanes(c, width)], tv.at[c], tsem.at[c])
 
     for c in range(NCH):
         for h in range(2):
@@ -161,7 +156,7 @@
         return rcopy(r, r, fbs.at[0], fbr.at[0], to_b)
 
     def b1(c):
-        return rcopy(stat.at[c], a1.at[c], as1.at[c], ar1.at[c], to_b)
+        return rcopy(stat.at[c, 1 - core], a1.at[c], as1.at[c], ar1.at[c], to_b)
 
     plane = [to_x, to_y, to_xy]
     here = y * 2 + x
@@ -183,9 +178,13 @@
         r = a3.at[c, from_z[k]]
         return rcopy(r, r, as3.at[c, k], ar3.at[c, k], to_z[k])
 
+    def b4(c, half):
+        r = fin.at[c, half]
+        return rcopy(r, r, as4.at[c], ar4.at[c], to_b)
+
     def sum_second(c):
         b1(c).wait_recv()
-        a2[c, here] = stat[c] + a1[c]
+        a2[c, here] = stat[c, core] + a1[c]
         for k in range(3):
             b2_out(c, k).start()
 
@@ -196,10 +195,42 @@
         for k in range(3):
             b3_out(c, k).start()
 
+    def sum_fourth(c):
+        for k in range(3):
+            b3_in(c, k).wait_recv()
+        fin[c, core] = (a3[c, 0] + a3[c, 1]) + (a3[c, 2] + a3[c, 3])
+        b4(c, core).start()
+
     def sum_last(c):
-        for k in range(3):
-            b3_in(c, k).wait_recv()
-        return (a3[c, 0] + a3[c, 1]) + (a3[c, 2] + a3[c, 3])
+        b4(c, 1 - core).wait_recv()
+        return jnp.concatenate([fin[c, 0], fin[c, 1]], axis=1)
+
+    def v1(n):
+        return rcopy(kvec.at[n], k1.at[n], ks1.at[n], kr1.at[n], to_b)
+
+    def v2(n, slot, k):
+        return rcopy(k2.at[n, slot], k2.at[n, slot], ks2.at[n, k], kr2.at[n, k], plane[k])
+
+    def v3(n, slot, k):
+        return rcopy(k3.at[n, slot], k3.at[n, slot], ks3.at[n, k], kr3.at[n, k], to_z[k])
+
+    def vector_second(n):
+        v1(n).wait_recv()
+        k2[n, here] = kvec[n] + k1[n]
+        for k in range(3):
+            v2(n, here, k).start()
+
+    def vector_third(n):
+        for k in range(3):
+            v2(n, there[k], k).wait_recv()
+        k3[n, z] = (k2[n, 0] + k2[n, 1]) + (k2[n, 2] + k2[n, 3])
+        for k in range(3):
+            v3(n, z, k).start()
+
+    def vector_last(n):
+        for k in range(3):
+            v3(n, from_z[k], k).wait_recv()
+        return (k3[n, 0] + k3[n, 1]) + (k3[n, 2] + k3[n, 3])
 
     def softmax(i, ent):
         get_logits(i).wait()
@@ -215,7 +246,9 @@
         ids = ids_ref[pl.ds(i, 1), :]
         square = (lax.broadcasted_iota(jnp.int32, (LANES, LANES), 0) == ids).astype(f32)
         oh[lanes(i), :] = square.T.astype(bf16)
-        ohm[:, lanes(i)] = square[:16, :].astype(bf16)
+        per = LANES // BR
+        turned = jnp.broadcast_to(ids, (LANES, LANES)).astype(f32).T
+        idc[pl.ds(i * per, per)] = turned.reshape(per, BR, LANES)
         return 0
 
     def weights(i, _):
@@ -238,108 +271,159 @@
         for k in range(3):
             z_out(c, k).start()
 
-    def gather_tick(t):
-        def stage_one(c):
-            for k in range(3):
-                z_in(c, k).wait_recv()
-            for d in s1_out(c):
-                d.start()
-
-        def stage_two(c):
-            for d in s1_in(c):
-                d.wait_recv()
-            for d in s2_out(c):
-                d.start()
-
-        def stage_three(c):
-            for d in s2_in(c):
-                d.wait_recv()
-            s3_out(c).start()
-
-        for lag, stage in ((0, stage_one), (1, stage_two), (2, stage_three)):
-            if isinstance(t, int):
-                if 0 <= t - lag < NCH:
-                    stage(t - lag)
-            else:
-                pl.when(jnp.logical_and(t - lag >= 0, t - lag < NCH))(lambda s=stage, c=t - lag: s(c))
-
-    for k in range(3):
-        fz_in(k).wait_recv()
-    fx(x).start()
-    gather_tick(0)
+    def stage_z(c):
+        for k in range(3):
+            z_in(c, k).wait_recv()
+        for d in s1_out(c):
+            d.start()
+
+    def stage_1(c):
+        for d in s1_in(c):
+            d.wait_recv()
+        for d in s2_out(c):
+            d.start()
+
+    def stage_2(c):
+        for d in s2_in(c):
+            d.wait_recv()
+        s3_out(c).start()
+
+    def fold(v):
+        out = v[:, :LANES]
+        for k in range(1, v.shape[1] // LANES):
+            out = out + v[:, k * LANES : (k + 1) * LANES]
+        return out
+
+    def eighths(v):
+        return jnp.sum(v.reshape(v.shape[0] // 8, 8, v.shape[1]), axis=0)
+
     for c in range(NCH):
         gm = jnp.concatenate(
             [gene_ref[:, c * width : (c + 1) * width].astype(f32), jnp.zeros((LANES - n_slides, width), f32)], axis=0
         )
         gmb[c] = gm.astype(bf16)
-    ent = lax.fori_loop(0, tiles // 2, softmax, jnp.zeros((1, LANES), f32))
-    fx(1 - x).wait_recv()
-    fy(y).start()
-    gather_tick(1)
-    ent = lax.fori_loop(tiles // 2, tiles, softmax, ent)
-    fy(1 - y).wait_recv()
-    fs(core).start()
-    gather_tick(2)
-    lax.fori_loop(0, tiles, one_hot, 0)
-    fs(1 - core).wait_recv()
-    keepc[...] = jax.nn.sigmoid(fb[...].reshape(n_cells, LANES))
-    lax.fori_loop(0, tiles, weights, 0)
     sd[...] = jnp.zeros_like(sd)
     sp[...] = jnp.zeros_like(sp)
     st[...] = jnp.zeros_like(st)
-
-    def fold(v):
-        out = v[:, :LANES]
-        for k in range(1, v.shape[1] // LANES):
-            out = out + v[:, k * LANES : (k + 1) * LANES]
-        return out
-
-    def forward(c):
+    lax.fori_loop(0, tiles, one_hot, 0)
+
+    begins = [jnp.sum((ids_ref[...] < k).astype(jnp.int32)) for k in range(n_slides + 1)]
+    firsts = [jnp.minimum(lax.div(begins[k], BR), n_blocks - 1) for k in range(n_slides)]
+    lasts = [lax.div(jnp.maximum(begins[k + 1] - 1, 0), BR) for k in range(n_slides)]
+    slide16 = lax.broadcasted_iota(jnp.int32, (16, 8 * n_blocks), 0)
+    block16 = lax.div(lax.broadcasted_iota(jnp.int32, (16, 8 * n_blocks), 1), 8)
+    inner = jnp.zeros((16, 8 * n_blocks), f32)
+    for k in range(n_slides):
+        full = jnp.logical_and(block16 > firsts[k], block16 < lasts[k])
+        inner = jnp.where(jnp.logical_and(slide16 == k, full), 1.0, inner)
+    inner = inner.astype(bf16)
+    inner = jnp.concatenate([inner, inner], axis=1)
+    slide8 = lax.broadcasted_iota(jnp.int32, (8, width), 0)
+
+    def gene_sums(c, products, number, at_row):
+        sums = []
+        for n in range(number):
+            bh, bl = split(blocks[n])
+            sums.append(mm(inner, jnp.concatenate([bh, bl], axis=0))[:8, :])
+        for k in range(n_slides):
+            parts = [jnp.zeros((8, width), f32)] * number
+            for block, counts in ((firsts[k], None), (lasts[k], lasts[k] != firsts[k])):
+                own = idc[block] == float(k)
+                if counts is not None:
+                    own = jnp.logical_and(own, counts)
+                own = own.astype(f32)
+                own = jnp.concatenate([own] * (width // LANES), axis=1)
+                for n, prod in enumerate(products(c, block)):
+                    parts[n] = parts[n] + eighths(prod * own)
+            for n in range(number):
+                line = jnp.sum(parts[n], axis=0, keepdims=True)
+                sums[n] = sums[n] + jnp.where(slide8 == k, line, 0.0)
+        for n in range(number):
+            for h in range(2):
+                stat[c, h, at_row + n * 8 : at_row + (n + 1) * 8, :] = sums[n][:, h * LANES : (h + 1) * LANES]
+
+    def of_target(c, r):
+        tgt = tv[c, r]
+        return (tgt * tgt,)
+
+    def of_both(c, r):
+        pred, tgt = pv[c, r], tv[c, r]
+        return pred * tgt, pred * pred
+
+    def by_rows(c, products, spots_of):
+        def rows_of(r, _):
+            at = pl.ds(pl.multiple_of(r * BR, BR), BR)
+            to = pl.ds(pl.multiple_of(r * 8, 8), 8)
+            sees = seen[at, :]
+            for n, (prod, spot) in enumerate(zip(products(c, r), spots_of)):
+                spot[at, :] += fold(sees * prod)
+                blocks[n, to, :] = eighths(prod)
+            return 0
+
+        lax.fori_loop(0, n_blocks, rows_of, 0, unroll=2)
+
+    def target_sums(c, _):
+        seen[...] = mm(oh[...], gmb[c])
+        by_rows(c, of_target, (st,))
+        gene_sums(c, of_target, 1, 16)
+        return 0
+
+    def predict(c):
         s3_in(c).wait_recv()
-        get_target(c).wait()
         whole = jnp.concatenate([buf[c, h].reshape(n_cells, LANES) for h in range(2)], axis=1)
         high, low = split(whole)
         chi[c] = high
         clo[c] = low
-
-        def rows_of(r, sums):
-            at = pl.ds(pl.multiple_of(r * TR, TR), TR)
-            wh, wl = thi[at, :], tlo[at, :]
-            ch, cl = chi[c], clo[c]
-            pred = mm(jnp.concatenate([wh, wl, wh], axis=1), jnp.concatenate([ch, ch, cl], axis=0))
-            pv[c, at, :] = pred
-            tgt = tv[c, at, :]
-            seen = mm(oh[at, :], gmb[c])
-            who = ohm[:, at]
-            who = jnp.concatenate([who, who], axis=1)
-            out = []
-            for prod, spot in ((pred * tgt, sd), (pred * pred, sp), (tgt * tgt, st)):
-                spot[at, :] += fold(seen * prod)
-                ph, plo = split(prod)
-                out.append(mm(who, jnp.concatenate([ph, plo], axis=0)))
-            return tuple(a + b for a, b in zip(sums, out))
-
-        zero = jnp.zeros((16, width), f32)
-        sums = lax.fori_loop(0, n_tiles, rows_of, (zero, zero, zero))
-        for k in range(3):
-            stat[c, k * 8 : (k + 1) * 8, :] = sums[k][:8, :]
-        put_pred(c).start()
-
-    zero8 = jnp.zeros((8, width), f32)
-
-    def middle(t, _):
-        gather_tick(t)
-        c = t - 3
-        forward(c)
-        stat[c, 24:32, :] = zero8
+        wh, wl = thi[...], tlo[...]
+        pred = mm(jnp.concatenate([wh, wl, wh], axis=1), jnp.concatenate([high, high, low], axis=0))
+        pv[c] = pred.reshape(n_blocks, BR, width)
+        seen[...] = mm(oh[...], gmb[c])
+
+    def predicted_sums(c):
+        by_rows(c, of_both, (sd, sp))
+        gene_sums(c, of_both, 2, 0)
+
+    ent = lax.fori_loop(0, tiles // 2, softmax, jnp.zeros((1, LANES), f32))
+    for k in range(3):
+        fz_in(k).wait_recv()
+    fx(x).start()
+    stage_z(0)
+    ent = lax.fori_loop(tiles // 2, tiles, softmax, ent)
+    fx(1 - x).wait_recv()
+    fy(y).start()
+    stage_z(1)
+    stage_1(0)
+    for c in range(NCH):
+        get_target(c).wait()
+    lax.fori_loop(0, 3, target_sums, 0)
+    fy(1 - y).wait_recv()
+    fs(core).start()
+    stage_z(2)
+    stage_1(1)
+    lax.fori_loop(3, 6, target_sums, 0)
+    stage_z(3)
+    stage_2(0)
+    fs(1 - core).wait_recv()
+    keepc[...] = jax.nn.sigmoid(fb[...].reshape(n_cells, LANES))
+    lax.fori_loop(0, tiles, weights, 0)
+    stage_1(2)
+    lax.fori_loop(6, NCH, target_sums, 0)
+
+    def gather_tick(t, _):
+        c = t - 4
+        pl.when(t < NCH)(lambda: stage_z(t))
+        pl.when(t - 3 < NCH)(lambda: stage_2(t - 3))
+        predict(c)
+        pl.when(t - 1 < NCH)(lambda: stage_1(t - 1))
+        pl.when(c >= 1)(lambda: sum_second(c - 1))
+        pl.when(c >= 3)(lambda: sum_third(c - 3))
+        predicted_sums(c)
+        pl.when(c >= 5)(lambda: sum_fourth(c - 5))
         b1(c).start()
-        pl.when(c >= 1)(lambda: sum_second(c - 1))
-        pl.when(c >= 2)(lambda: sum_third(c - 2))
         return 0
 
-    lax.fori_loop(3, NCH + 2, middle, 0)
+    lax.fori_loop(4, NCH + 4, gather_tick, 0)
     last = NCH - 1
-    forward(last)
 
     def spot_rows(i, _):
         for k, ref in enumerate((sd, sp, st)):
@@ -384,10 +468,11 @@
         extra = jnp.where(lane8 == k, jnp.sum(value, axis=1, keepdims=True), extra)
     extra = jnp.where(jnp.logical_and(lane8 == 3, iota8 == 0), -jnp.sum(scos), extra)
     extra = jnp.where(jnp.logical_and(lane8 == 4, iota8 == 0), -jnp.sum(ent), extra)
-    stat[last, 24:32, :] = jnp.concatenate([extra] + [zero] * (width // LANES - 1), axis=1)
-    b1(last).start()
-    sum_second(last - 1)
+    kvec[0] = extra
+    v1(0).start()
+    sum_second(last)
     sum_third(last - 2)
+    sum_fourth(last - 4)
 
     gacc[...] = jnp.zeros_like(gacc)
     gw[...] = jnp.zeros_like(gw)
@@ -440,7 +525,6 @@
 
     def backward(c):
         total = sum_last(c)
-        gtot[c] = total
         dot_s, pp_s, tt_s = total[0:8], total[8:16], total[16:24]
         gm = gene_ref[:, lanes(c, width)].astype(f32)
         gscale = gm * lax.rsqrt(pp_s + eps) * lax.rsqrt(tt_s + eps)
@@ -455,58 +539,68 @@
             coefs.append(
                 jnp.concatenate([high.astype(f32), low.astype(f32), gm, gm, pad], axis=0).astype(bf16)
             )
-
-        def rows_of(r, _):
-            at = pl.ds(pl.multiple_of(r * TR, TR), TR)
-            grad = mm(l2[at, :], coefs[1]) * pv[c, at, :] - mm(l1[at, :], coefs[0]) * tv[c, at, :]
-            high, low = split(grad)
-            gph[at, :] = high
-            gpl[at, :] = low
-            return 0
-
-        lax.fori_loop(0, n_tiles, rows_of, 0)
-
-        def cells_of(r, _):
-            at = pl.ds(pl.multiple_of(r * LANES, LANES), LANES)
-            wh, wl = whi[at, :], wlo[at, :]
-            gh, gl = gph[...], gpl[...]
-            out = mm(jnp.concatenate([wh, wl, wh], axis=1), jnp.concatenate([gh, gh, gl], axis=0))
-            for h in range(2):
-                part[c, h, r] = out[:, h * LANES : (h + 1) * LANES].reshape(2, 2, 2, 16, LANES)
-            return 0
-
-        lax.fori_loop(0, n_cells // LANES, cells_of, 0)
+        slot = lax.rem(c, HELD)
+        grad = mm(l2[...], coefs[1]) * pv[c].reshape(spots, width) - mm(l1[...], coefs[0]) * tv[c].reshape(spots, width)
+        gh, gl = split(grad)
+        gph[slot] = gh
+        gpl[slot] = gl
+        wh, wl = whi[...], wlo[...]
+        gh, gl = gph[slot], gpl[slot]
+        out = mm(jnp.concatenate([wh, wl, wh], axis=1), jnp.concatenate([gh, gh, gl], axis=0))
+        for h in range(2):
+            part[c, h] = out[:, h * LANES : (h + 1) * LANES].reshape(4, 2, 2, 2, 16, LANES)
         scatter_sib(c).start()
 
-        def spots_of(r, _):
-            at = pl.ds(pl.multiple_of(r * TR, TR), TR)
-            ch, cl = chi[c], clo[c]
-            gh, gl = gph[at, :], gpl[at, :]
-            out = mm_nt(jnp.concatenate([ch, cl, ch], axis=1), jnp.concatenate([gh, gh, gl], axis=1))
-            for h in range(TR // LANES):
-                gw[r * (TR // LANES) + h] += out[:, h * LANES : (h + 1) * LANES]
-            return 0
-
-        lax.fori_loop(0, n_tiles, spots_of, 0)
+    def spot_part(c):
+        slot = lax.rem(c, HELD)
+        ch, cl = chi[c], clo[c]
+        gh, gl = gph[slot], gpl[slot]
+        out = mm_nt(jnp.concatenate([ch, cl, ch], axis=1), jnp.concatenate([gh, gh, gl], axis=1))
+        for i in range(tiles):
+            gw[i] += out[:, i * LANES : (i + 1) * LANES]
 
     def back_tick(t, _):
+        pl.when(t >= 3)(lambda: sc2(t - 3))
         backward(t)
-        pl.when(t == 0)(lambda: sum_second(last))
-        pl.when(t == 0)(lambda: sum_third(last - 1))
-        pl.when(t == 1)(lambda: sum_third(last))
         pl.when(t >= 1)(lambda: sc1(t - 1))
-        pl.when(t >= 2)(lambda: sc2(t - 2))
-        pl.when(t >= 3)(lambda: sc3(t - 3))
-        pl.when(t >= 4)(lambda: sc4(t - 4))
+        pl.when(t >= 4)(lambda: sc3(t - 4))
+
+        @pl.when(t == 0)
+        def _():
+            vector_second(0)
+            sum_third(last - 1)
+            sum_fourth(last - 3)
+
+        @pl.when(t == 1)
+        def _():
+            sum_third(last)
+            sum_fourth(last - 2)
+
+        @pl.when(t == 2)
+        def _():
+            vector_third(0)
+            sum_fourth(last - 1)
+
+        @pl.when(t == 3)
+        def _():
+            sum_fourth(last)
+
+        pl.when(t >= 3)(lambda: spot_part(t - 3))
+        pl.when(t >= 6)(lambda: sc4(t - 6))
         return 0
 
     lax.fori_loop(0, NCH, back_tick, 0)
     sc1(last)
+    spot_part(last - 2)
+    sc2(last - 2)
+    sc3(last - 3)
+    spot_part(last - 1)
     sc2(last - 1)
-    sc3(last - 2)
-
-    sums_s = gtot[last, 24:32, :LANES]
-    mass_s, wsum_s, logsum_s = sums_s[:, 0:1], sums_s[:, 1:2], sums_s[:, 2:3]
+    spot_part(last)
+
+    sums_s = vector_last(0)
+    sums_ref[...] = sums_s
+    mass_s, wsum_s = sums_s[:, 0:1], sums_s[:, 1:2]
     kp[...] = jnp.zeros_like(kp)
 
     def finish(i, _):
@@ -515,13 +609,8 @@
         mass_at = jnp.sum(mine * mass_s, axis=0, keepdims=True)
         wsum_at = jnp.sum(mine * wsum_s, axis=0, keepdims=True)
         gmass = -(dens_ref[at, :] / wsum_at) / mass[at, :] + 1.0 / mass_at
-        prob = lg[i]
-        grad = gw[i] + gmass
-        kp[...] += prob * grad
-        grad = keepc[...] * grad
-        middle_ = jnp.sum(prob * grad, axis=0, keepdims=True)
-        gw[i] = prob * (grad - middle_)
-        put_glog(i).start()
+        gmass_ref[at, :] = gmass
+        kp[...] += lg[i] * (gw[i] + gmass)
         return 0
 
     lax.fori_loop(0, tiles, finish, 0)
@@ -531,41 +620,109 @@
         rows_k.append(jnp.sum(kp[q * LANES : (q + 1) * LANES, :].T, axis=0, keepdims=True))
         rows_keep.append(keepc[q * LANES : (q + 1) * LANES, :].T[0:1, :])
     blank = jnp.zeros((8 - quarter, LANES), f32)
-    kvec[...] = jnp.concatenate(rows_k + [blank], axis=0)
+    kvec[1] = jnp.concatenate(rows_k + [blank], axis=0)
+    v1(1).start()
     keep = jnp.concatenate(rows_keep, axis=0)
-
-    k1_copy = rcopy(kvec, k1, ks1.at[0], kr1.at[0], to_b)
-
-    def k2_copy(slot, k):
-        return rcopy(k2.at[slot], k2.at[slot], ks2.at[k], kr2.at[k], plane[k])
-
-    def k3_copy(slot, k):
-        return rcopy(k3.at[slot], k3.at[slot], ks3.at[k], kr3.at[k], to_z[k])
-
-    k1_copy.start()
+    keep_ref[...] = jnp.concatenate([keep, blank], axis=0)
+
     sc2(last)
+    sc3(last - 2)
     sc3(last - 1)
-    sc4(last - 3)
-    k1_copy.wait_recv()
-    k2[here] = kvec[...] + k1[...]
-    for k in range(3):
-        k2_copy(here, k).start()
+    vector_second(1)
     sc3(last)
-    sc4(last - 2)
-    for k in range(3):
-        k2_copy(there[k], k).wait_recv()
-    k3[z] = (k2[0] + k2[1]) + (k2[2] + k2[3])
-    for k in range(3):
-        k3_copy(z, k).start()
+    for c in range(NCH - 6, NCH - 3):
+        sc4(c)
+    vector_third(1)
+    for c in range(NCH - 3, NCH):
+        sc4(c)
 
     ok = mask_ref[...].astype(f32)
     count = jnp.sum(ok * keep)
     target_count = n_cells // 4
-    count_term = jnp.abs(count - target_count) / n_cells
+
+    total = vector_last(1)[:quarter, :]
+    off = count - target_count
+    sign = jnp.where(off > 0, 1.0, jnp.where(off < 0, -1.0, 0.0))
+    total = total + ok * (sign + 1.0 - 2.0 * keep) / n_cells
+    total = total * keep * (1.0 - keep)
+    kvec_out = jnp.concatenate([total, blank], axis=0)
+    dev = wide * 4 + narrow
+    picked = jnp.sum(jnp.where(iota8 == lax.div(dev, 8), kvec_out, 0.0), axis=0, keepdims=True)
+    picked = pltpu.roll(picked, lax.rem(LANES - lax.rem(dev, 8) * 16, LANES), 1)
+    gfilt_ref[...] = picked
+
+    def leave(c, _):
+        for k in range(3):
+            z_out(c, k).wait_send()
+            b2_out(c, k).wait_send()
+            b3_out(c, k).wait_send()
+            scatter_z(c, k).wait_send()
+        for d in s1_out(c) + s2_out(c) + scatter_one(c) + scatter_two(c):
+            d.wait_send()
+        s3_out(c).wait_send()
+        b1(c).wait_send()
+        b4(c, core).wait_send()
+        scatter_sib(c).wait_send()
+        return 0
+
+    lax.fori_loop(0, NCH, leave, 0)
+    for k in range(3):
+        fz_out(k).wait_send()
+        for n in range(2):
+            v2(n, here, k).wait_send()
+            v3(n, z, k).wait_send()
+    fx(x).wait_send()
+    fy(y).wait_send()
+    fs(core).wait_send()
+    for n in range(2):
+        v1(n).wait_send()
+
+
+def finish_kernel(
+    pv, lg, gw, keepc, gmass_ref, gacc, sums_ref, keep_ref, gcos_in, scos_in, gfilt_in, gcell_in, mask_ref,
+    terms_ref, reg_ref, pred_hbm, gcos_ref, scos_ref, glog_hbm, gfilt_ref, gcell_ref,
+    psem, osem,
+):
+    width = pv.shape[3]
+    tiles, n_cells = lg.shape[:2]
+
+    def lanes(i, w=LANES):
+        return pl.ds(pl.multiple_of(i * w, w), w)
+
+    def put_pred(c):
+        return pltpu.make_async_copy(pv.at[c], pred_hbm.at[:, :, lanes(c, width)], psem.at[c])
+
+    def put_glog(i):
+        return pltpu.make_async_copy(gw.at[i], glog_hbm.at[:, lanes(i)], osem.at[i])
+
+    for c in range(NCH):
+        put_pred(c).start()
+
+    def finish(i, _):
+        grad = keepc[...] * (gw[i] + gmass_ref[pl.ds(i, 1), :])
+        prob = lg[i]
+        gw[i] = prob * (grad - jnp.sum(prob * grad, axis=0, keepdims=True))
+        put_glog(i).start()
+        return 0
+
+    lax.fori_loop(0, tiles, finish, 0)
+    gcos_ref[...] = gcos_in[...]
+    scos_ref[...] = scos_in[...]
+    gcell_ref[...] = gcell_in[...]
+    gfilt_ref[...] = gfilt_in[:, : gfilt_ref.shape[1]]
+
+    sums_s = sums_ref[...]
+    mass_s, wsum_s, logsum_s = sums_s[:, 0:1], sums_s[:, 1:2], sums_s[:, 2:3]
+    row = lax.broadcasted_iota(jnp.int32, sums_s.shape, 0)
+    lane = lax.broadcasted_iota(jnp.int32, sums_s.shape, 1)
+    keep = keep_ref[: n_cells // LANES, :]
+    ok = mask_ref[...].astype(f32)
+    count = jnp.sum(ok * keep)
+    count_term = jnp.abs(count - n_cells // 4) / n_cells
     binarity = jnp.sum(ok * (keep - keep * keep)) / n_cells
     gene_loss = -jnp.sum(gacc[...])
-    spot_loss = jnp.sum(jnp.where(jnp.logical_and(lane8 == 3, iota8 == 0), sums_s, 0.0))
-    entropy = jnp.sum(jnp.where(jnp.logical_and(lane8 == 4, iota8 == 0), sums_s, 0.0)) / (spots * 32)
+    spot_loss = jnp.sum(jnp.where(jnp.logical_and(lane == 3, row == 0), sums_s, 0.0))
+    entropy = jnp.sum(jnp.where(jnp.logical_and(lane == 4, row == 0), sums_s, 0.0)) / (tiles * LANES * 32)
     kl = jnp.sum(logsum_s / wsum_s + jnp.log(mass_s) - jnp.log(wsum_s))
     terms_ref[0] = gene_loss + spot_loss + kl + count_term + binarity
     terms_ref[1] = gene_loss
@@ -574,47 +731,10 @@
     reg_ref[1] = count_term
     reg_ref[2] = binarity
     reg_ref[3] = entropy
-
-    sc4(last - 1)
-    for k in range(3):
-        k3_copy(from_z[k], k).wait_recv()
-    total = ((k3[0] + k3[1]) + (k3[2] + k3[3]))[:quarter, :]
-    off = count - target_count
-    sign = jnp.where(off > 0, 1.0, jnp.where(off < 0, -1.0, 0.0))
-    total = total + ok * (sign + 1.0 - 2.0 * keep) / n_cells
-    total = total * keep * (1.0 - keep)
-    kvec_out = jnp.concatenate([total, blank], axis=0)
-    dev = wide * 4 + narrow
-    picked = jnp.sum(jnp.where(iota8 == lax.div(dev, 8), kvec_out, 0.0), axis=0, keepdims=True)
-    picked = pltpu.roll(picked, lax.rem(LANES - lax.rem(dev, 8) * 16, LANES), 1)
-    gfilt_ref[...] = picked[:, :16]
-    sc4(last)
-
-    def leave(c, _):
-        for k in range(3):
-            z_out(c, k).wait_send()
-            b2_out(c, k).wait_send()
-            b3_out(c, k).wait_send()
-            scatter_z(c, k).wait_send()
-        for d in s1_out(c) + s2_out(c) + scatter_one(c) + scatter_two(c):
-            d.wait_send()
-        s3_out(c).wait_send()
-        b1(c).wait_send()
-        scatter_sib(c).wait_send()
-        put_pred(c).wait()
-        return 0
-
-    lax.fori_loop(0, NCH, leave, 0)
     for i in range(tiles):
         put_glog(i).wait()
-    for k in range(3):
-        fz_out(k).wait_send()
-        k2_copy(here, k).wait_send()
-        k3_copy(z, k).wait_send()
-    fx(x).wait_send()
-    fy(y).wait_send()
-    fs(core).wait_send()
-    k1_copy.wait_send()
+    for c in range(NCH):
+        put_pred(c).wait()
 
 
 def fused(logits, filt, cells, cell_mask, gene_mask, slide_ids, target, density):
@@ -629,14 +749,11 @@
     scalars = pl.BlockSpec(memory_space=pltpu.SMEM)
     ring = (4, 2, 2, 2, 16, LANES)
     scratch = [
-        vmem((tiles, n_cells, LANES), f32),
-        vmem((NCH, spots, width), f32),
-        vmem((NCH, spots, width), f32),
+        vmem((NCH, spots // BR, BR, width), f32),
         vmem((NCH, 2) + ring, f32),
         vmem((NCH, n_cells, width), bf16),
         vmem((NCH, n_cells, width), bf16),
         vmem(ring, f32),
-        vmem((n_cells, LANES), f32),
         vmem((n_cells, LANES), f32),
         vmem((n_cells, spots), bf16),
         vmem((n_cells, spots), bf16),
@@ -644,28 +761,28 @@
         vmem((spots, n_cells), bf16),
         vmem((NCH, LANES, width), bf16),
         vmem((spots, LANES), bf16),
-        vmem((16, spots), bf16),
         vmem((spots, LANES), bf16),
         vmem((spots, LANES), bf16),
+        vmem((spots // BR, BR, LANES), f32),
+        vmem((spots, width), f32),
+        vmem((2, spots * 8 // BR, width), f32),
         vmem((spots, LANES), f32),
         vmem((spots, LANES), f32),
         vmem((spots, LANES), f32),
         vmem((8, LANES), f32),
         vmem((5, 8, LANES), f32),
-        vmem((spots, width), bf16),
-        vmem((spots, width), bf16),
-        vmem((tiles, n_cells, LANES), f32),
+        vmem((HELD, spots, width), bf16),
+        vmem((HELD, spots, width), bf16),
         vmem((n_cells, LANES), f32),
-        vmem((NCH, 32, width), f32),
-        vmem((NCH, 32, width), f32),
-        vmem((NCH, 4, 32, width), f32),
-        vmem((NCH, 4, 32, width), f32),
-        vmem((NCH, 32, width), f32),
-        vmem((8, width), f32),
-        vmem((8, LANES), f32),
-        vmem((8, LANES), f32),
-        vmem((4, 8, LANES), f32),
-        vmem((4, 8, LANES), f32),
+        vmem((NCH, 2, 24, LANES), f32),
+        vmem((NCH, 24, LANES), f32),
+        vmem((NCH, 4, 24, LANES), f32),
+        vmem((NCH, 4, 24, LANES), f32),
+        vmem((NCH, 2, 24, LANES), f32),
+        vmem((2, 8, LANES), f32),
+        vmem((2, 8, LANES), f32),
+        vmem((2, 4, 8, LANES), f32),
+        vmem((2, 4, 8, LANES), f32),
         vmem((NCH, 2) + ring, f32),
         vmem((NCH, 2, 4, 2, 2, 16, LANES), f32),
         vmem((NCH, 2, 4, 2, 2, 16, LANES), f32),
@@ -674,37 +791,60 @@
         vmem((NCH, 2, 4, 16, LANES), f32),
         vmem((NCH, 2, 4, 16, LANES), f32),
         vmem((NCH, 3, 2, 16, LANES), f32),
-        dma((NCH, 2)), dma((NCH,)), dma((NCH,)), dma((tiles,)),
+        dma((NCH, 2)), dma((NCH,)), dma((tiles,)),
         dma((NCH, 3)), dma((NCH, 3)), dma((NCH, 2)), dma((NCH, 2)), dma((NCH, 2)), dma((NCH, 2)), dma((NCH,)), dma((NCH,)),
         dma((3,)), dma((3,)), dma((1,)), dma((1,)), dma((1,)), dma((1,)), dma((1,)), dma((1,)),
-        dma((NCH,)), dma((NCH,)), dma((NCH, 3)), dma((NCH, 3)), dma((NCH, 3)), dma((NCH, 3)),
-        dma((1,)), dma((1,)), dma((3,)), dma((3,)), dma((3,)), dma((3,)),
+        dma((NCH,)), dma((NCH,)), dma((NCH, 3)), dma((NCH, 3)), dma((NCH, 3)), dma((NCH, 3)), dma((NCH,)), dma((NCH,)),
+        dma((2,)), dma((2,)), dma((2, 3)), dma((2, 3)), dma((2, 3)), dma((2, 3)),
         dma((NCH,)), dma((NCH,)), dma((NCH, 2)), dma((NCH, 2)), dma((NCH, 2)), dma((NCH, 2)), dma((NCH, 3)), dma((NCH, 3)),
     ]
+    mask = cell_mask.reshape(n_cells // LANES, LANES)
+    held = (
+        vmem((NCH, spots // BR, BR, width), f32),
+        vmem((tiles, n_cells, LANES), f32),
+        vmem((tiles, n_cells, LANES), f32),
+        vmem((n_cells, LANES), f32),
+        vmem((tiles, LANES), f32),
+        vmem((8, width), f32),
+        vmem((8, LANES), f32),
+        vmem((8, LANES), f32),
+        vmem((n_slides, genes), f32),
+        vmem((tiles, LANES), f32),
+        vmem((1, LANES), f32),
+        vmem((own, genes), f32),
+    )
+    between = pl.pallas_call(
+        fused_kernel,
+        out_shape=held,
+        in_specs=[anywhere, scalars, anywhere, inside, inside, inside, anywhere, inside],
+        out_specs=(inside,) * len(held),
+        scratch_shapes=scratch,
+        compiler_params=pltpu.CompilerParams(
+            collective_id=0, has_side_effects=True, vmem_limit_bytes=50 << 20
+        ),
+    )(
+        logits, filt, cells, mask, gene_mask,
+        slide_ids.reshape(tiles, LANES), target.reshape(spots // BR, BR, genes), density.reshape(tiles, LANES),
+    )
     out = pl.pallas_call(
-        fused_kernel,
+        finish_kernel,
         out_shape=(
             jax.ShapeDtypeStruct((3,), f32),
             jax.ShapeDtypeStruct((4,), f32),
-            jax.ShapeDtypeStruct((spots, genes), f32),
+            jax.ShapeDtypeStruct((spots // BR, BR, genes), f32),
             jax.ShapeDtypeStruct((n_slides, genes), f32),
             jax.ShapeDtypeStruct((tiles, LANES), f32),
             jax.ShapeDtypeStruct((n_cells, spots), f32),
             jax.ShapeDtypeStruct((1, own), f32),
             jax.ShapeDtypeStruct((own, genes), f32),
         ),
-        in_specs=[anywhere, scalars, anywhere, inside, inside, inside, anywhere, inside],
+        in_specs=[inside] * (len(held) + 1),
         out_specs=(scalars, scalars, anywhere, inside, inside, anywhere, inside, inside),
-        scratch_shapes=scratch,
-        compiler_params=pltpu.CompilerParams(
-            collective_id=0, has_side_effects=True, vmem_limit_bytes=60 << 20
-        ),
-    )(
-        logits, filt, cells, cell_mask.reshape(n_cells // LANES, LANES), gene_mask,
-        slide_ids.reshape(tiles, LANES), target, density.reshape(tiles, LANES),
-    )
+        scratch_shapes=[dma((NCH,)), dma((tiles,))],
+        compiler_params=pltpu.CompilerParams(vmem_limit_bytes=24 << 20),
+    )(*between, mask)
     terms, reg, pred, gcos, scos, glog, gfilt, gcell = out
-    return terms, reg, pred, gcos, scos.reshape(spots), glog, gfilt.reshape(own), gcell
+    return terms, reg, pred.reshape(spots, genes), gcos, scos.reshape(spots), glog, gfilt.reshape(own), gcell
 
 
 def per_slide(onehot, values):

time: 120 us -> 86.4 us (0.72)
  Pallas kernels: 105 us -> 85.6 us
  local copies, waits for them, and re-layouts: 14 us -> 0.01 us
    pallas_call x1 -> x2, Pallas kernels: 105 us -> 85.6 us  [the longest x1 80.9 us: fused(): pl.pallas_call(fused_kernel, out_shape=held, in_specs=[anywhere, scalars,...]
    unnamed x18 -> x2, local copies, waits for them, and re-layouts: 14 us -> 0.01 us
where the time goes in v1:
time: 86.4 us; the launch traced here: 86.3 us
  Pallas kernels  85.6 us (99%)
    pallas_call x1, Pallas kernels, fused(): pl.pallas_call(fused_kernel, out_shape=held, in_specs=[anywhere, scalars,...  80.9 us
    pallas_call x1, Pallas kernels, fused(): pl.pallas_call(finish_kernel, out_shape=(jax.ShapeDtypeStruct((3,), f32),...  4.75 us

profile of v1, /device:TPU:0, one launch (start us, length us, event | category | flops | bytes accessed | tf_op | source)
XLA Modules:
  0.0 86.3 jit_solution(6047183151534308543)
XLA Ops:
  0.6 0.0 copy-start
  0.6 80.9 %shard_map.143 = (f32[8,32,32,256]{3,2,1,0:T(8,128)S(1)}, f32[8,512,128]{2,1,0:T(8,128)S(1)}, f32[8,512,128]{2,1,0:T(8,128)S(1)}, f32[512,128]{1,0:T(8,128)S(1)}...) custom-call(f32[512,1024]{1,0:T(8,128)} %logits_hbm.1, ...), custom_call_target="tpu_custom_call" | custom-call | tf_op jit(solution)/shard_map/pallas_call | solution.py:816
  81.5 0.0 copy-done
  81.5 4.8 %shard_map.144 = (f32[3]{0:T(128)}, f32[4]{0:T(128)}, f32[32,32,2048]{2,1,0:T(8,128)}, f32[8,2048]{1,0:T(8,128)}, f32[8,128]{1,0:T(8,128)}, /*index=5*/f32[512,1...) custom-call(f32[8,32,32,256]{3,2,1,0:T(8,128)S(1)} %get-tuple-element.28.pv, f32[8,512,128]{2,1,0:T(8,128)S(1)} %get-tuple-element.29.lg, ...), custom_call_target="tpu_custom_call" | custom-call | tf_op jit(solution)/shard_map/pallas_call | solution.py:829
Async XLA Ops:
  0.6 80.9 %copy-start = (s32[512]{0:T(512)S(1)}, s32[512]{0:T(512)}, u32[]{:S(2)}) copy-start(s32[512]{0:T(512)} %param.11) | copy-start | bytes 6148

commit v2 on v1

--- a/solution.py
+++ b/solution.py
@@ -12,7 +12,7 @@
 LANES = 128
 NCH = 8
 BR = 32
-HELD = 4
+GR = 256
 
 
 def split(value):
@@ -32,7 +32,7 @@
     logits_hbm, filt_ref, cells_hbm, mask_ref, gene_ref, ids_ref, target_hbm, dens_ref,
     pv, lg, gw, keepc, gmass_ref, gacc, sums_ref, keep_ref, gcos_ref, scos_ref, gfilt_ref, gcell_ref,
     tv, buf, chi, clo, fb, valid, whi, wlo, thi, tlo, gmb, oh, l1, l2,
-    idc, seen, blocks, sd, sp, st, mass, rows, gph, gpl, kp,
+    idc, blocks, sd, sp, st, mass, rows, gph, gpl, kp,
     stat, a1, a2, a3, fin, kvec, k1, k2, k3,
     part, rb, sb, r1, tt_, r2, qq, r3,
     lsem, tsem, osem,
@@ -348,22 +348,21 @@
 
     def of_both(c, r):
         pred, tgt = pv[c, r], tv[c, r]
-        return pred * tgt, pred * pred
+        return pred * tgt, jnp.where(tgt > 0.0, pred * pred, 0.0)
 
     def by_rows(c, products, spots_of):
-        def rows_of(r, _):
-            at = pl.ds(pl.multiple_of(r * BR, BR), BR)
-            to = pl.ds(pl.multiple_of(r * 8, 8), 8)
-            sees = seen[at, :]
+        for r in range(n_blocks):
+            at = slice(r * BR, (r + 1) * BR)
             for n, (prod, spot) in enumerate(zip(products(c, r), spots_of)):
-                spot[at, :] += fold(sees * prod)
-                blocks[n, to, :] = eighths(prod)
-            return 0
-
-        lax.fori_loop(0, n_blocks, rows_of, 0, unroll=2)
+                spot[at, :] += fold(prod)
+                blocks[n, r * 8 : (r + 1) * 8, :] = eighths(prod)
 
     def target_sums(c, _):
-        seen[...] = mm(oh[...], gmb[c])
+        per = GR // BR
+        for n in range(spots // GR):
+            sees = mm(oh[n * GR : (n + 1) * GR, :], gmb[c]).reshape(per, BR, width)
+            for r in range(per):
+                tv[c, n * per + r] = sees[r] * tv[c, n * per + r]
         by_rows(c, of_target, (st,))
         gene_sums(c, of_target, 1, 16)
         return 0
@@ -377,7 +376,6 @@
         wh, wl = thi[...], tlo[...]
         pred = mm(jnp.concatenate([wh, wl, wh], axis=1), jnp.concatenate([high, high, low], axis=0))
         pv[c] = pred.reshape(n_blocks, BR, width)
-        seen[...] = mm(oh[...], gmb[c])
 
     def predicted_sums(c):
         by_rows(c, of_both, (sd, sp))
@@ -414,12 +412,12 @@
         pl.when(t < NCH)(lambda: stage_z(t))
         pl.when(t - 3 < NCH)(lambda: stage_2(t - 3))
         predict(c)
+        predicted_sums(c)
+        b1(c).start()
         pl.when(t - 1 < NCH)(lambda: stage_1(t - 1))
         pl.when(c >= 1)(lambda: sum_second(c - 1))
         pl.when(c >= 3)(lambda: sum_third(c - 3))
-        predicted_sums(c)
         pl.when(c >= 5)(lambda: sum_fourth(c - 5))
-        b1(c).start()
         return 0
 
     lax.fori_loop(4, NCH + 4, gather_tick, 0)
@@ -475,7 +473,6 @@
     sum_fourth(last - 4)
 
     gacc[...] = jnp.zeros_like(gacc)
-    gw[...] = jnp.zeros_like(gw)
 
     def scatter_sib(c):
         return rcopy(part.at[c, :, :, :, :, 1 - core], rb.at[c], cbs.at[c], cbr.at[c], to_b)
@@ -539,25 +536,30 @@
             coefs.append(
                 jnp.concatenate([high.astype(f32), low.astype(f32), gm, gm, pad], axis=0).astype(bf16)
             )
-        slot = lax.rem(c, HELD)
-        grad = mm(l2[...], coefs[1]) * pv[c].reshape(spots, width) - mm(l1[...], coefs[0]) * tv[c].reshape(spots, width)
-        gh, gl = split(grad)
-        gph[slot] = gh
-        gpl[slot] = gl
+        per = GR // BR
+        for n in range(spots // GR):
+            at = slice(n * GR, (n + 1) * GR)
+            own = slice(n * per, (n + 1) * per)
+            pred, tgt = pv[c, own].reshape(GR, width), tv[c, own].reshape(GR, width)
+            gh, gl = split(mm(l2[at, :], coefs[1]) * pred - mm(l1[at, :], coefs[0]) * tgt)
+            gph[c, at, :] = gh
+            gpl[c, at, :] = gl
         wh, wl = whi[...], wlo[...]
-        gh, gl = gph[slot], gpl[slot]
+        gh, gl = gph[c], gpl[c]
         out = mm(jnp.concatenate([wh, wl, wh], axis=1), jnp.concatenate([gh, gh, gl], axis=0))
         for h in range(2):
             part[c, h] = out[:, h * LANES : (h + 1) * LANES].reshape(4, 2, 2, 2, 16, LANES)
         scatter_sib(c).start()
 
-    def spot_part(c):
-        slot = lax.rem(c, HELD)
-        ch, cl = chi[c], clo[c]
-        gh, gl = gph[slot], gpl[slot]
-        out = mm_nt(jnp.concatenate([ch, cl, ch], axis=1), jnp.concatenate([gh, gh, gl], axis=1))
-        for i in range(tiles):
-            gw[i] += out[:, i * LANES : (i + 1) * LANES]
+    def spot_part(n):
+        at = pl.ds(n * GR, GR)
+        left = [chi[c] for c in range(NCH)]
+        left = left + [clo[c] for c in range(NCH)] + left
+        right = [gph[c, at, :] for c in range(NCH)]
+        right = right + right + [gpl[c, at, :] for c in range(NCH)]
+        out = mm_nt(jnp.concatenate(left, axis=1), jnp.concatenate(right, axis=1))
+        for h in range(GR // LANES):
+            gw[n * (GR // LANES) + h] = out[:, h * LANES : (h + 1) * LANES]
 
     def back_tick(t, _):
         pl.when(t >= 3)(lambda: sc2(t - 3))
@@ -585,71 +587,90 @@
         def _():
             sum_fourth(last)
 
-        pl.when(t >= 3)(lambda: spot_part(t - 3))
+        @pl.when(t == 4)
+        def _():
+            slide_totals()
+
+        @pl.when(t == 5)
+        def _():
+            vector_second(1)
+
+        @pl.when(t == 7)
+        def _():
+            vector_third(1)
+
         pl.when(t >= 6)(lambda: sc4(t - 6))
         return 0
 
+    quarter = n_cells // LANES
+    blank = jnp.zeros((8 - quarter, LANES), f32)
+
+    def slide_totals():
+        sums_s = vector_last(0)
+        sums_ref[...] = sums_s
+        mass_s, wsum_s = sums_s[:, 0:1], sums_s[:, 1:2]
+        kp[...] = jnp.zeros_like(kp)
+
+        def by_mass(i, _):
+            at = pl.ds(i, 1)
+            mine = (iota8 == ids_ref[at, :]).astype(f32)
+            mass_at = jnp.sum(mine * mass_s, axis=0, keepdims=True)
+            wsum_at = jnp.sum(mine * wsum_s, axis=0, keepdims=True)
+            gmass = -(dens_ref[at, :] / wsum_at) / mass[at, :] + 1.0 / mass_at
+            gmass_ref[at, :] = gmass
+            kp[...] += lg[i] * gmass
+            return 0
+
+        lax.fori_loop(0, tiles, by_mass, 0)
+        kp[...] = kp[...] * keepc[...]
+        rows_k = [jnp.sum(kp[q * LANES : (q + 1) * LANES, :].T, axis=0, keepdims=True) for q in range(quarter)]
+        kvec[1] = jnp.concatenate(rows_k + [blank], axis=0)
+        v1(1).start()
+
     lax.fori_loop(0, NCH, back_tick, 0)
     sc1(last)
-    spot_part(last - 2)
+    sc3(last - 3)
     sc2(last - 2)
-    sc3(last - 3)
-    spot_part(last - 1)
+    spot_part(0)
+    sc3(last - 2)
     sc2(last - 1)
-    spot_part(last)
-
-    sums_s = vector_last(0)
-    sums_ref[...] = sums_s
-    mass_s, wsum_s = sums_s[:, 0:1], sums_s[:, 1:2]
-    kp[...] = jnp.zeros_like(kp)
-
-    def finish(i, _):
-        at = pl.ds(i, 1)
-        mine = (iota8 == ids_ref[at, :]).astype(f32)
-        mass_at = jnp.sum(mine * mass_s, axis=0, keepdims=True)
-        wsum_at = jnp.sum(mine * wsum_s, axis=0, keepdims=True)
-        gmass = -(dens_ref[at, :] / wsum_at) / mass[at, :] + 1.0 / mass_at
-        gmass_ref[at, :] = gmass
-        kp[...] += lg[i] * (gw[i] + gmass)
-        return 0
-
-    lax.fori_loop(0, tiles, finish, 0)
-    quarter = n_cells // LANES
-    rows_k, rows_keep = [], []
-    for q in range(quarter):
-        rows_k.append(jnp.sum(kp[q * LANES : (q + 1) * LANES, :].T, axis=0, keepdims=True))
-        rows_keep.append(keepc[q * LANES : (q + 1) * LANES, :].T[0:1, :])
-    blank = jnp.zeros((8 - quarter, LANES), f32)
-    kvec[1] = jnp.concatenate(rows_k + [blank], axis=0)
-    v1(1).start()
-    keep = jnp.concatenate(rows_keep, axis=0)
-    keep_ref[...] = jnp.concatenate([keep, blank], axis=0)
-
     sc2(last)
-    sc3(last - 2)
+    spot_part(1)
     sc3(last - 1)
-    vector_second(1)
     sc3(last)
     for c in range(NCH - 6, NCH - 3):
         sc4(c)
-    vector_third(1)
-    for c in range(NCH - 3, NCH):
-        sc4(c)
-
+    spot_part(2)
+    spot_part(3)
+
+    rows_keep = [keepc[q * LANES : (q + 1) * LANES, :].T[0:1, :] for q in range(quarter)]
+    keep = jnp.concatenate(rows_keep, axis=0)
+    keep_ref[...] = jnp.concatenate([keep, blank], axis=0)
     ok = mask_ref[...].astype(f32)
     count = jnp.sum(ok * keep)
     target_count = n_cells // 4
-
     total = vector_last(1)[:quarter, :]
     off = count - target_count
     sign = jnp.where(off > 0, 1.0, jnp.where(off < 0, -1.0, 0.0))
-    total = total + ok * (sign + 1.0 - 2.0 * keep) / n_cells
-    total = total * keep * (1.0 - keep)
-    kvec_out = jnp.concatenate([total, blank], axis=0)
     dev = wide * 4 + narrow
-    picked = jnp.sum(jnp.where(iota8 == lax.div(dev, 8), kvec_out, 0.0), axis=0, keepdims=True)
-    picked = pltpu.roll(picked, lax.rem(LANES - lax.rem(dev, 8) * 16, LANES), 1)
-    gfilt_ref[...] = picked
+
+    def own_lanes(rows_q):
+        picked = jnp.concatenate([rows_q, blank], axis=0)
+        picked = jnp.sum(jnp.where(iota8 == lax.div(dev, 8), picked, 0.0), axis=0, keepdims=True)
+        return pltpu.roll(picked, lax.rem(LANES - lax.rem(dev, 8) * 16, LANES), 1)
+
+    own_keep = own_lanes(keep)
+    own_rest = own_lanes(total + ok * keep * (sign + 1.0 - 2.0 * keep) / n_cells)
+    for c in range(NCH - 3, NCH):
+        sc4(c)
+    along = jnp.zeros((16, LANES), f32)
+    for c in range(NCH):
+        for h in range(2):
+            at = (c * 2 + h) * LANES
+            along = along + buf[c, h, z, y, x, core] * gcell_ref[:, at : at + LANES]
+    along = jnp.concatenate([along, jnp.zeros((LANES - 16, LANES), f32)], axis=0)
+    along = jnp.sum(along.T, axis=0, keepdims=True)
+    gfilt_ref[...] = (along + own_rest) * (1.0 - own_keep)
 
     def leave(c, _):
         for k in range(3):
@@ -764,15 +785,14 @@
         vmem((spots, LANES), bf16),
         vmem((spots, LANES), bf16),
         vmem((spots // BR, BR, LANES), f32),
-        vmem((spots, width), f32),
         vmem((2, spots * 8 // BR, width), f32),
         vmem((spots, LANES), f32),
         vmem((spots, LANES), f32),
         vmem((spots, LANES), f32),
         vmem((8, LANES), f32),
         vmem((5, 8, LANES), f32),
-        vmem((HELD, spots, width), bf16),
-        vmem((HELD, spots, width), bf16),
+        vmem((NCH, spots, width), bf16),
+        vmem((NCH, spots, width), bf16),
         vmem((n_cells, LANES), f32),
         vmem((NCH, 2, 24, LANES), f32),
         vmem((NCH, 24, LANES), f32),

time: 86.4 us -> 82.3 us (0.953)
  Pallas kernels: 85.6 us -> 81.5 us
    pallas_call x1, Pallas kernels: 80.9 us -> 76.7 us  [fused(): pl.pallas_call(fused_kernel, out_shape=held, in_specs=[anywhere, scalars,...]
where the time goes in v2:
time: 82.3 us; the launch traced here: 82.1 us
  Pallas kernels  81.5 us (99%)
    pallas_call x1, Pallas kernels, fused(): pl.pallas_call(fused_kernel, out_shape=held, in_specs=[anywhere, scalars,...  76.7 us
    pallas_call x1, Pallas kernels, fused(): pl.pallas_call(finish_kernel, out_shape=(jax.ShapeDtypeStruct((3,), f32),...  4.75 us

profile of v2, /device:TPU:0, one launch (start us, length us, event | category | flops | bytes accessed | tf_op | source)
XLA Modules:
  0.0 82.1 jit_solution(1904043733557133434)
XLA Ops:
  0.6 0.0 copy-start
  0.6 76.7 %shard_map.143 = (f32[8,32,32,256]{3,2,1,0:T(8,128)S(1)}, f32[8,512,128]{2,1,0:T(8,128)S(1)}, f32[8,512,128]{2,1,0:T(8,128)S(1)}, f32[512,128]{1,0:T(8,128)S(1)}...) custom-call(f32[512,1024]{1,0:T(8,128)} %logits_hbm.1, ...), custom_call_target="tpu_custom_call" | custom-call | tf_op jit(solution)/shard_map/pallas_call | solution.py:836
  77.4 0.0 copy-done
  77.4 4.8 %shard_map.144 = (f32[3]{0:T(128)}, f32[4]{0:T(128)}, f32[32,32,2048]{2,1,0:T(8,128)}, f32[8,2048]{1,0:T(8,128)}, f32[8,128]{1,0:T(8,128)}, /*index=5*/f32[512,1...) custom-call(f32[8,32,32,256]{3,2,1,0:T(8,128)S(1)} %get-tuple-element.28.pv, f32[8,512,128]{2,1,0:T(8,128)S(1)} %get-tuple-element.29.lg, ...), custom_call_target="tpu_custom_call" | custom-call | tf_op jit(solution)/shard_map/pallas_call | solution.py:849
Async XLA Ops:
  0.6 76.7 %copy-start = (s32[512]{0:T(512)S(1)}, s32[512]{0:T(512)}, u32[]{:S(2)}) copy-start(s32[512]{0:T(512)} %param.11) | copy-start | bytes 6148

commit v3 on v2

--- a/solution.py
+++ b/solution.py
@@ -13,6 +13,7 @@
 NCH = 8
 BR = 32
 GR = 256
+AHEAD = 3
 
 
 def split(value):
@@ -30,20 +31,20 @@
 
 def fused_kernel(
     logits_hbm, filt_ref, cells_hbm, mask_ref, gene_ref, ids_ref, target_hbm, dens_ref,
-    pv, lg, gw, keepc, gmass_ref, gacc, sums_ref, keep_ref, gcos_ref, scos_ref, gfilt_ref, gcell_ref,
-    tv, buf, chi, clo, fb, valid, whi, wlo, thi, tlo, gmb, oh, l1, l2,
-    idc, blocks, sd, sp, st, mass, rows, gph, gpl, kp,
+    pv, gw, keep_ref, sums_ref, loss_ref, gcos_ref, scos_ref, gfilt_ref, gcell_ref,
+    lg, tv, buf, chi, clo, ownc, ownk, along, valid, keepc, whi, wlo, thi, tlo, gmb, oh, l1, l2, cf,
+    idc, blocks, sd, sp, st, mass, gmass, gph, gpl, kp,
     stat, a1, a2, a3, fin, kvec, k1, k2, k3,
     part, rb, sb, r1, tt_, r2, qq, r3,
     lsem, tsem, osem,
     zs, zr, xs, xr, ys, yr, bs, br,
-    fzs, fzr, fxs, fxr, fys, fyr, fbs, fbr,
     as1, ar1, as2, ar2, as3, ar3, as4, ar4,
     ks1, kr1, ks2, kr2, ks3, kr3,
     cbs, cbr, cxs, cxr, cys, cyr, czs, czr,
 ):
     n_cells = chi.shape[1]
     width = chi.shape[2]
+    last = NCH - 1
     n_blocks = tv.shape[1]
     spots = n_blocks * BR
     n_slides = gene_ref.shape[0]
@@ -66,10 +67,7 @@
     def lanes(i, w=LANES):
         return pl.ds(pl.multiple_of(i * w, w), w)
 
-    def own_cells(c, h):
-        return pltpu.make_async_copy(
-            cells_hbm.at[:, pl.ds((c * 2 + h) * LANES, LANES)], buf.at[c, h, z, y, x, core], lsem.at[c, h]
-        )
+    own_cells = pltpu.make_async_copy(cells_hbm, ownc, lsem.at[0])
 
     def get_logits(i):
         return pltpu.make_async_copy(logits_hbm.at[:, lanes(i)], lg.at[i], osem.at[i])
@@ -77,9 +75,7 @@
     def get_target(c):
         return pltpu.make_async_copy(target_hbm.at[:, :, lanes(c, width)], tv.at[c], tsem.at[c])
 
-    for c in range(NCH):
-        for h in range(2):
-            own_cells(c, h).start()
+    own_cells.start()
     for i in range(tiles):
         get_logits(i).start()
     for c in range(NCH):
@@ -89,11 +85,24 @@
     for dev in to_z + [to_x, to_y, to_xy, to_b]:
         pl.semaphore_signal(barrier, inc=1, device_id=dev, device_id_type=MESH)
 
+    iota8 = lax.broadcasted_iota(jnp.int32, (8, LANES), 0)
+    lane8 = lax.broadcasted_iota(jnp.int32, (8, LANES), 1)
     row16 = lax.broadcasted_iota(jnp.int32, (16, LANES), 0)
+    dev = wide * 4 + narrow
+    place = lane8 + iota8 * LANES - dev * 16
     mine = jnp.zeros((16, LANES), f32)
+    vector = jnp.zeros((8, LANES), f32)
     for r in range(16):
         mine = jnp.where(row16 == r, filt_ref[r], mine)
-    fb[z, y, x, core] = mine
+        vector = jnp.where(place == r, filt_ref[r], vector)
+    kvec[2] = vector
+    own_keep = jax.nn.sigmoid(mine)
+    ownk[...] = own_keep
+    along[...] = jnp.zeros_like(along)
+    own_cells.wait()
+    for c in range(NCH):
+        for h in range(2):
+            buf[c, h, z, y, x, core] = own_keep * ownc[:, (c * 2 + h) * LANES : (c * 2 + h + 1) * LANES]
     for q in range(n_cells // LANES):
         line = mask_ref[q : q + 1, :].astype(f32)
         valid[q * LANES : (q + 1) * LANES, :] = jnp.broadcast_to(line, (LANES, LANES)).T
@@ -135,26 +144,6 @@
         r = buf.at[c, :, :, :, :, 1 - core]
         return rcopy(r, r, bs.at[c], br.at[c], to_b)
 
-    def fz_out(k):
-        r = fb.at[z, y, x, core]
-        return rcopy(r, r, fzs.at[k], fzr.at[k], to_z[k])
-
-    def fz_in(k):
-        r = fb.at[from_z[k], y, x, core]
-        return rcopy(r, r, fzs.at[k], fzr.at[k], to_z[k])
-
-    def fx(at):
-        r = fb.at[:, y, at, core]
-        return rcopy(r, r, fxs.at[0], fxr.at[0], to_x)
-
-    def fy(at):
-        r = fb.at[:, at, :, core]
-        return rcopy(r, r, fys.at[0], fyr.at[0], to_y)
-
-    def fs(at):
-        r = fb.at[:, :, :, at]
-        return rcopy(r, r, fbs.at[0], fbr.at[0], to_b)
-
     def b1(c):
         return rcopy(stat.at[c, 1 - core], a1.at[c], as1.at[c], ar1.at[c], to_b)
 
@@ -203,7 +192,6 @@
 
     def sum_last(c):
         b4(c, 1 - core).wait_recv()
-        return jnp.concatenate([fin[c, 0], fin[c, 1]], axis=1)
 
     def v1(n):
         return rcopy(kvec.at[n], k1.at[n], ks1.at[n], kr1.at[n], to_b)
@@ -240,6 +228,12 @@
         total = jnp.sum(expo, axis=0, keepdims=True)
         prob = expo * (1.0 / total)
         lg[i] = prob
+        high, low = split(prob)
+        whi[:, lanes(i)] = high
+        wlo[:, lanes(i)] = low
+        high, low = split(prob.T)
+        thi[lanes(i), :] = high
+        tlo[lanes(i), :] = low
         return ent + jnp.sum(prob * (value - top - jnp.log(total)), axis=0, keepdims=True)
 
     def one_hot(i, _):
@@ -251,25 +245,13 @@
         idc[pl.ds(i * per, per)] = turned.reshape(per, BR, LANES)
         return 0
 
-    def weights(i, _):
-        w = lg[i] * keepc[...]
-        mass[pl.ds(i, 1), :] = jnp.sum(w, axis=0, keepdims=True)
-        high, low = split(w)
-        whi[:, lanes(i)] = high
-        wlo[:, lanes(i)] = low
-        turned = w.T
-        high, low = split(turned)
-        thi[lanes(i), :] = high
-        tlo[lanes(i), :] = low
-        return 0
-
-    for k in range(3):
-        fz_out(k).start()
-    for c in range(NCH):
-        for h in range(2):
-            own_cells(c, h).wait()
+    def leave_z(c):
         for k in range(3):
             z_out(c, k).start()
+
+    for c in range(AHEAD):
+        leave_z(c)
+    v1(2).start()
 
     def stage_z(c):
         for k in range(3):
@@ -381,98 +363,93 @@
         by_rows(c, of_both, (sd, sp))
         gene_sums(c, of_both, 2, 0)
 
+    def slide_sums():
+        keep_rows = jax.nn.sigmoid(vector_last(2))
+        keep_ref[...] = keep_rows
+        for q in range(quarter):
+            line = jnp.broadcast_to(keep_rows[q : q + 1, :], (LANES, LANES))
+            keepc[q * LANES : (q + 1) * LANES, :] = line.T
+
+        def by_tile(i, sums):
+            at = pl.ds(i, 1)
+            line = jnp.sum(lg[i] * keepc[...], axis=0, keepdims=True)
+            mass[at, :] = line
+            dens = dens_ref[at, :]
+            mine = (iota8 == ids_ref[at, :]).astype(f32)
+            terms = (line, dens, dens * (jnp.log(dens) - jnp.log(line)))
+            return tuple(a + mine * b for a, b in zip(sums, terms))
+
+        blank = jnp.zeros((8, LANES), f32)
+        totals = lax.fori_loop(0, tiles, by_tile, (blank, blank, blank))
+        for k, value in enumerate(totals):
+            blank = jnp.where(lane8 == k, jnp.sum(value, axis=1, keepdims=True), blank)
+        kvec[0] = blank
+        v1(0).start()
+
+    quarter = n_cells // LANES
     ent = lax.fori_loop(0, tiles // 2, softmax, jnp.zeros((1, LANES), f32))
-    for k in range(3):
-        fz_in(k).wait_recv()
-    fx(x).start()
     stage_z(0)
+    leave_z(AHEAD)
+    vector_second(2)
     ent = lax.fori_loop(tiles // 2, tiles, softmax, ent)
-    fx(1 - x).wait_recv()
-    fy(y).start()
     stage_z(1)
-    stage_1(0)
+    leave_z(AHEAD + 1)
     for c in range(NCH):
         get_target(c).wait()
     lax.fori_loop(0, 3, target_sums, 0)
-    fy(1 - y).wait_recv()
-    fs(core).start()
     stage_z(2)
-    stage_1(1)
+    leave_z(AHEAD + 2)
+    stage_1(0)
+    vector_third(2)
     lax.fori_loop(3, 6, target_sums, 0)
     stage_z(3)
+    leave_z(AHEAD + 3)
+    stage_1(1)
+    lax.fori_loop(6, NCH, target_sums, 0)
+    stage_z(4)
+    leave_z(AHEAD + 4)
     stage_2(0)
-    fs(1 - core).wait_recv()
-    keepc[...] = jax.nn.sigmoid(fb[...].reshape(n_cells, LANES))
-    lax.fori_loop(0, tiles, weights, 0)
     stage_1(2)
-    lax.fori_loop(6, NCH, target_sums, 0)
+    slide_sums()
 
     def gather_tick(t, _):
-        c = t - 4
+        c = t - 5
         pl.when(t < NCH)(lambda: stage_z(t))
-        pl.when(t - 3 < NCH)(lambda: stage_2(t - 3))
+        pl.when(t + AHEAD < NCH)(lambda: leave_z(t + AHEAD))
+        pl.when(t - 4 < NCH)(lambda: stage_2(t - 4))
+        pl.when(t - 2 < NCH)(lambda: stage_1(t - 2))
         predict(c)
         predicted_sums(c)
         b1(c).start()
-        pl.when(t - 1 < NCH)(lambda: stage_1(t - 1))
+        pl.when(c == 0)(lambda: vector_second(0))
+        pl.when(c == 2)(lambda: vector_third(0))
         pl.when(c >= 1)(lambda: sum_second(c - 1))
         pl.when(c >= 3)(lambda: sum_third(c - 3))
-        pl.when(c >= 5)(lambda: sum_fourth(c - 5))
+        pl.when(c >= 6)(lambda: sum_fourth(c - 6))
         return 0
 
-    lax.fori_loop(4, NCH + 4, gather_tick, 0)
-    last = NCH - 1
+    lax.fori_loop(5, NCH + 5, gather_tick, 0)
+
+    lane128 = lax.broadcasted_iota(jnp.int32, (LANES, LANES), 1)
+    slide_of_lane = lax.rem(lane128, 8).astype(f32)
 
     def spot_rows(i, _):
-        for k, ref in enumerate((sd, sp, st)):
-            rows[k, pl.ds(i, 1), :] = jnp.sum(ref[lanes(i), :].T, axis=0, keepdims=True)
+        at = lanes(i)
+        sdot, spp, stt = [jnp.sum(ref[at, :], axis=1, keepdims=True) for ref in (sd, sp, st)]
+        scale = lax.rsqrt(spp + eps) * lax.rsqrt(stt + eps)
+        sd[at, :] = jnp.broadcast_to(sdot * scale, (LANES, LANES))
+        per = LANES // BR
+        own = jnp.logical_and(idc[pl.ds(i * per, per)].reshape(LANES, LANES) == slide_of_lane, lane128 < 32)
+        for ref, value in ((l1, scale), (l2, scale * (sdot / (spp + eps)))):
+            high, low = split(value)
+            value = jnp.where(lane128 < 16, 1.0, jnp.where(lane128 < 24, high.astype(f32), low.astype(f32)))
+            ref[at, :] = jnp.where(own, value, 0.0).astype(bf16)
         return 0
 
     lax.fori_loop(0, tiles, spot_rows, 0)
-    sdot, spp, stt = rows[0], rows[1], rows[2]
-    scale = lax.rsqrt(spp + eps) * lax.rsqrt(stt + eps)
-    scos = sdot * scale
-    scos_ref[...] = scos
-    shrink = scale * (sdot / (spp + eps))
-    for k, value in ((0, scale), (1, shrink)):
-        high, low = split(value)
-        rows[2 * k] = high.astype(f32)
-        rows[2 * k + 1] = low.astype(f32)
-    dens = dens_ref[...]
-    mass_row = mass[...]
-    rows[4] = dens * (jnp.log(dens) - jnp.log(mass_row))
-
-    iota8 = lax.broadcasted_iota(jnp.int32, (8, LANES), 0)
-    lane8 = lax.broadcasted_iota(jnp.int32, (8, LANES), 1)
-
-    def coef_rows(i, sums):
-        mine = (iota8 == ids_ref[pl.ds(i, 1), :]).astype(f32)
-        pad = jnp.zeros((LANES - 32, LANES), f32)
-        at = pl.ds(i, 1)
-        for k, ref in ((0, l1), (1, l2)):
-            ref[lanes(i), :] = jnp.concatenate(
-                [mine, mine, mine * rows[2 * k, at, :], mine * rows[2 * k + 1, at, :], pad], axis=0
-            ).T.astype(bf16)
-        return (
-            sums[0] + mine * mass[at, :],
-            sums[1] + mine * dens_ref[at, :],
-            sums[2] + mine * rows[4, at, :],
-        )
-
-    zero = jnp.zeros((8, LANES), f32)
-    totals = lax.fori_loop(0, tiles, coef_rows, (zero, zero, zero))
-    extra = zero
-    for k, value in enumerate(totals):
-        extra = jnp.where(lane8 == k, jnp.sum(value, axis=1, keepdims=True), extra)
-    extra = jnp.where(jnp.logical_and(lane8 == 3, iota8 == 0), -jnp.sum(scos), extra)
-    extra = jnp.where(jnp.logical_and(lane8 == 4, iota8 == 0), -jnp.sum(ent), extra)
-    kvec[0] = extra
-    v1(0).start()
     sum_second(last)
     sum_third(last - 2)
-    sum_fourth(last - 4)
-
-    gacc[...] = jnp.zeros_like(gacc)
+    sum_fourth(last - 5)
 
     def scatter_sib(c):
         return rcopy(part.at[c, :, :, :, :, 1 - core], rb.at[c], cbs.at[c], cbr.at[c], to_b)
@@ -518,30 +495,32 @@
         for k in range(3):
             scatter_z(c, k).wait_recv()
         for h in range(2):
-            gcell_ref[:, lanes(c * 2 + h)] = (qq[c, h, z] + r3[c, 0, h]) + (r3[c, 1, h] + r3[c, 2, h])
-
-    def backward(c):
-        total = sum_last(c)
+            at = lanes(c * 2 + h)
+            total = (qq[c, h, z] + r3[c, 0, h]) + (r3[c, 1, h] + r3[c, 2, h])
+            gcell_ref[:, at] = total * ownk[...]
+            along[...] += total * ownc[:, at]
+
+    def gene_coefs(c):
+        total = jnp.concatenate([fin[c, 0], fin[c, 1]], axis=1)
         dot_s, pp_s, tt_s = total[0:8], total[8:16], total[16:24]
         gm = gene_ref[:, lanes(c, width)].astype(f32)
         gscale = gm * lax.rsqrt(pp_s + eps) * lax.rsqrt(tt_s + eps)
-        gcos = dot_s * gscale
-        gcos_ref[:, lanes(c, width)] = gcos
-        gacc[...] += gcos
+        gcos_ref[:, lanes(c, width)] = dot_s * gscale
         gshrink = gscale * (dot_s / (pp_s + eps))
         pad = jnp.zeros((LANES - 32, width), f32)
-        coefs = []
-        for value in (gscale, gshrink):
+        for n, value in enumerate((gscale, gshrink)):
             high, low = split(value)
-            coefs.append(
-                jnp.concatenate([high.astype(f32), low.astype(f32), gm, gm, pad], axis=0).astype(bf16)
-            )
+            high, low = high.astype(f32), low.astype(f32)
+            cf[lax.rem(c, 2), n] = jnp.concatenate([high, low, gm, gm, pad], axis=0).astype(bf16)
+
+    def backward(c):
+        slot = lax.rem(c, 2)
         per = GR // BR
         for n in range(spots // GR):
             at = slice(n * GR, (n + 1) * GR)
             own = slice(n * per, (n + 1) * per)
             pred, tgt = pv[c, own].reshape(GR, width), tv[c, own].reshape(GR, width)
-            gh, gl = split(mm(l2[at, :], coefs[1]) * pred - mm(l1[at, :], coefs[0]) * tgt)
+            gh, gl = split(mm(l2[at, :], cf[slot, 1]) * pred - mm(l1[at, :], cf[slot, 0]) * tgt)
             gph[c, at, :] = gh
             gpl[c, at, :] = gl
         wh, wl = whi[...], wlo[...]
@@ -549,6 +528,7 @@
         out = mm(jnp.concatenate([wh, wl, wh], axis=1), jnp.concatenate([gh, gh, gl], axis=0))
         for h in range(2):
             part[c, h] = out[:, h * LANES : (h + 1) * LANES].reshape(4, 2, 2, 2, 16, LANES)
+        gene_coefs(jnp.minimum(c + 1, last))
         scatter_sib(c).start()
 
     def spot_part(n):
@@ -559,33 +539,19 @@
         right = right + right + [gpl[c, at, :] for c in range(NCH)]
         out = mm_nt(jnp.concatenate(left, axis=1), jnp.concatenate(right, axis=1))
         for h in range(GR // LANES):
-            gw[n * (GR // LANES) + h] = out[:, h * LANES : (h + 1) * LANES]
+            i = n * (GR // LANES) + h
+            grad = out[:, h * LANES : (h + 1) * LANES] + keepc[...] * gmass[i : i + 1, :]
+            prob = lg[i]
+            gw[i] = prob * (grad - jnp.sum(prob * grad, axis=0, keepdims=True))
 
     def back_tick(t, _):
         pl.when(t >= 3)(lambda: sc2(t - 3))
+        pl.when(t < last)(lambda: sum_last(t + 1))
         backward(t)
         pl.when(t >= 1)(lambda: sc1(t - 1))
         pl.when(t >= 4)(lambda: sc3(t - 4))
-
-        @pl.when(t == 0)
-        def _():
-            vector_second(0)
-            sum_third(last - 1)
-            sum_fourth(last - 3)
-
-        @pl.when(t == 1)
-        def _():
-            sum_third(last)
-            sum_fourth(last - 2)
-
-        @pl.when(t == 2)
-        def _():
-            vector_third(0)
-            sum_fourth(last - 1)
-
-        @pl.when(t == 3)
-        def _():
-            sum_fourth(last)
+        pl.when(t <= 1)(lambda: sum_third(last - 1 + t))
+        pl.when(t <= 4)(lambda: sum_fourth(last - 4 + t))
 
         @pl.when(t == 4)
         def _():
@@ -601,9 +567,6 @@
 
         pl.when(t >= 6)(lambda: sc4(t - 6))
         return 0
-
-    quarter = n_cells // LANES
-    blank = jnp.zeros((8 - quarter, LANES), f32)
 
     def slide_totals():
         sums_s = vector_last(0)
@@ -611,22 +574,26 @@
         mass_s, wsum_s = sums_s[:, 0:1], sums_s[:, 1:2]
         kp[...] = jnp.zeros_like(kp)
 
-        def by_mass(i, _):
+        def by_mass(i, total):
             at = pl.ds(i, 1)
             mine = (iota8 == ids_ref[at, :]).astype(f32)
             mass_at = jnp.sum(mine * mass_s, axis=0, keepdims=True)
             wsum_at = jnp.sum(mine * wsum_s, axis=0, keepdims=True)
-            gmass = -(dens_ref[at, :] / wsum_at) / mass[at, :] + 1.0 / mass_at
-            gmass_ref[at, :] = gmass
-            kp[...] += lg[i] * gmass
-            return 0
-
-        lax.fori_loop(0, tiles, by_mass, 0)
-        kp[...] = kp[...] * keepc[...]
+            line = -(dens_ref[at, :] / wsum_at) / mass[at, :] + 1.0 / mass_at
+            gmass[at, :] = line
+            kp[...] += lg[i] * line
+            spot = sd[lanes(i), :].T[0:1, :]
+            scos_ref[at, :] = spot
+            return total + spot
+
+        total = lax.fori_loop(0, tiles, by_mass, jnp.zeros((1, LANES), f32))
         rows_k = [jnp.sum(kp[q * LANES : (q + 1) * LANES, :].T, axis=0, keepdims=True) for q in range(quarter)]
-        kvec[1] = jnp.concatenate(rows_k + [blank], axis=0)
+        rows_k = rows_k + [-total, -ent, jnp.zeros((6 - quarter, LANES), f32)]
+        kvec[1] = jnp.concatenate(rows_k, axis=0)
         v1(1).start()
 
+    sum_last(0)
+    gene_coefs(0)
     lax.fori_loop(0, NCH, back_tick, 0)
     sc1(last)
     sc3(last - 3)
@@ -643,34 +610,25 @@
     spot_part(2)
     spot_part(3)
 
-    rows_keep = [keepc[q * LANES : (q + 1) * LANES, :].T[0:1, :] for q in range(quarter)]
-    keep = jnp.concatenate(rows_keep, axis=0)
-    keep_ref[...] = jnp.concatenate([keep, blank], axis=0)
-    ok = mask_ref[...].astype(f32)
-    count = jnp.sum(ok * keep)
-    target_count = n_cells // 4
-    total = vector_last(1)[:quarter, :]
-    off = count - target_count
+    keep = keep_ref[...]
+    ok = jnp.concatenate([mask_ref[...].astype(f32), jnp.zeros((8 - quarter, LANES), f32)], axis=0)
+    off = jnp.sum(ok * keep) - n_cells // 4
     sign = jnp.where(off > 0, 1.0, jnp.where(off < 0, -1.0, 0.0))
-    dev = wide * 4 + narrow
-
-    def own_lanes(rows_q):
-        picked = jnp.concatenate([rows_q, blank], axis=0)
-        picked = jnp.sum(jnp.where(iota8 == lax.div(dev, 8), picked, 0.0), axis=0, keepdims=True)
+    totals = vector_last(1)
+    loss_ref[...] = totals
+    rest = totals + ok * (sign + 1.0 - 2.0 * keep) / n_cells
+
+    def own_lanes(value):
+        picked = jnp.sum(jnp.where(iota8 == lax.div(dev, 8), value, 0.0), axis=0, keepdims=True)
         return pltpu.roll(picked, lax.rem(LANES - lax.rem(dev, 8) * 16, LANES), 1)
 
-    own_keep = own_lanes(keep)
-    own_rest = own_lanes(total + ok * keep * (sign + 1.0 - 2.0 * keep) / n_cells)
+    keep = own_lanes(keep)
+    rest = own_lanes(rest)
     for c in range(NCH - 3, NCH):
         sc4(c)
-    along = jnp.zeros((16, LANES), f32)
-    for c in range(NCH):
-        for h in range(2):
-            at = (c * 2 + h) * LANES
-            along = along + buf[c, h, z, y, x, core] * gcell_ref[:, at : at + LANES]
-    along = jnp.concatenate([along, jnp.zeros((LANES - 16, LANES), f32)], axis=0)
-    along = jnp.sum(along.T, axis=0, keepdims=True)
-    gfilt_ref[...] = (along + own_rest) * (1.0 - own_keep)
+    genes_part = jnp.concatenate([along[...], jnp.zeros((LANES - 16, LANES), f32)], axis=0)
+    genes_part = jnp.sum(genes_part.T, axis=0, keepdims=True)
+    gfilt_ref[...] = ((genes_part + rest) * keep * (1.0 - keep))[:, : gfilt_ref.shape[1]]
 
     def leave(c, _):
         for k in range(3):
@@ -687,63 +645,47 @@
         return 0
 
     lax.fori_loop(0, NCH, leave, 0)
-    for k in range(3):
-        fz_out(k).wait_send()
-        for n in range(2):
+    for n in range(3):
+        v1(n).wait_send()
+        for k in range(3):
             v2(n, here, k).wait_send()
             v3(n, z, k).wait_send()
-    fx(x).wait_send()
-    fy(y).wait_send()
-    fs(core).wait_send()
-    for n in range(2):
-        v1(n).wait_send()
 
 
 def finish_kernel(
-    pv, lg, gw, keepc, gmass_ref, gacc, sums_ref, keep_ref, gcos_in, scos_in, gfilt_in, gcell_in, mask_ref,
-    terms_ref, reg_ref, pred_hbm, gcos_ref, scos_ref, glog_hbm, gfilt_ref, gcell_ref,
-    psem, osem,
+    pv, gw, keep_ref, sums_ref, loss_ref, gcos_in, scos_in, gfilt_in, gcell_in, mask_ref,
+    terms_hbm, reg_hbm, pred_hbm, gcos_hbm, scos_hbm, glog_hbm, gfilt_hbm, gcell_hbm,
+    terms_ref, reg_ref, psem, osem, rsem,
 ):
     width = pv.shape[3]
-    tiles, n_cells = lg.shape[:2]
-
-    def lanes(i, w=LANES):
-        return pl.ds(pl.multiple_of(i * w, w), w)
+    tiles, n_cells = gw.shape[:2]
+    quarter = n_cells // LANES
 
     def put_pred(c):
-        return pltpu.make_async_copy(pv.at[c], pred_hbm.at[:, :, lanes(c, width)], psem.at[c])
+        return pltpu.make_async_copy(pv.at[c], pred_hbm.at[:, :, c * width : (c + 1) * width], psem.at[c])
 
     def put_glog(i):
-        return pltpu.make_async_copy(gw.at[i], glog_hbm.at[:, lanes(i)], osem.at[i])
+        return pltpu.make_async_copy(gw.at[i], glog_hbm.at[:, i * LANES : (i + 1) * LANES], osem.at[i])
 
     for c in range(NCH):
         put_pred(c).start()
-
-    def finish(i, _):
-        grad = keepc[...] * (gw[i] + gmass_ref[pl.ds(i, 1), :])
-        prob = lg[i]
-        gw[i] = prob * (grad - jnp.sum(prob * grad, axis=0, keepdims=True))
+    for i in range(tiles):
         put_glog(i).start()
-        return 0
-
-    lax.fori_loop(0, tiles, finish, 0)
-    gcos_ref[...] = gcos_in[...]
-    scos_ref[...] = scos_in[...]
-    gcell_ref[...] = gcell_in[...]
-    gfilt_ref[...] = gfilt_in[:, : gfilt_ref.shape[1]]
+    pairs = [(gcos_in, gcos_hbm), (scos_in, scos_hbm), (gcell_in, gcell_hbm), (gfilt_in, gfilt_hbm)]
+    rest = [pltpu.make_async_copy(a, b, rsem.at[k]) for k, (a, b) in enumerate(pairs)]
+    for copy in rest:
+        copy.start()
 
     sums_s = sums_ref[...]
     mass_s, wsum_s, logsum_s = sums_s[:, 0:1], sums_s[:, 1:2], sums_s[:, 2:3]
-    row = lax.broadcasted_iota(jnp.int32, sums_s.shape, 0)
-    lane = lax.broadcasted_iota(jnp.int32, sums_s.shape, 1)
-    keep = keep_ref[: n_cells // LANES, :]
+    keep = keep_ref[:quarter, :]
     ok = mask_ref[...].astype(f32)
     count = jnp.sum(ok * keep)
     count_term = jnp.abs(count - n_cells // 4) / n_cells
     binarity = jnp.sum(ok * (keep - keep * keep)) / n_cells
-    gene_loss = -jnp.sum(gacc[...])
-    spot_loss = jnp.sum(jnp.where(jnp.logical_and(lane == 3, row == 0), sums_s, 0.0))
-    entropy = jnp.sum(jnp.where(jnp.logical_and(lane == 4, row == 0), sums_s, 0.0)) / (tiles * LANES * 32)
+    gene_loss = -jnp.sum(gcos_in[...])
+    spot_loss = jnp.sum(loss_ref[quarter : quarter + 1, :])
+    entropy = jnp.sum(loss_ref[quarter + 1 : quarter + 2, :]) / (tiles * LANES * 32)
     kl = jnp.sum(logsum_s / wsum_s + jnp.log(mass_s) - jnp.log(wsum_s))
     terms_ref[0] = gene_loss + spot_loss + kl + count_term + binarity
     terms_ref[1] = gene_loss
@@ -752,6 +694,11 @@
     reg_ref[1] = count_term
     reg_ref[2] = binarity
     reg_ref[3] = entropy
+    for k, (a, b) in enumerate(((terms_ref, terms_hbm), (reg_ref, reg_hbm))):
+        rest.append(pltpu.make_async_copy(a, b, rsem.at[len(pairs) + k]))
+        rest[-1].start()
+    for copy in rest:
+        copy.wait()
     for i in range(tiles):
         put_glog(i).wait()
     for c in range(NCH):
@@ -770,11 +717,15 @@
     scalars = pl.BlockSpec(memory_space=pltpu.SMEM)
     ring = (4, 2, 2, 2, 16, LANES)
     scratch = [
+        vmem((tiles, n_cells, LANES), f32),
         vmem((NCH, spots // BR, BR, width), f32),
         vmem((NCH, 2) + ring, f32),
         vmem((NCH, n_cells, width), bf16),
         vmem((NCH, n_cells, width), bf16),
-        vmem(ring, f32),
+        vmem((own, genes), f32),
+        vmem((own, LANES), f32),
+        vmem((own, LANES), f32),
+        vmem((n_cells, LANES), f32),
         vmem((n_cells, LANES), f32),
         vmem((n_cells, spots), bf16),
         vmem((n_cells, spots), bf16),
@@ -784,13 +735,14 @@
         vmem((spots, LANES), bf16),
         vmem((spots, LANES), bf16),
         vmem((spots, LANES), bf16),
+        vmem((2, 2, LANES, width), bf16),
         vmem((spots // BR, BR, LANES), f32),
         vmem((2, spots * 8 // BR, width), f32),
         vmem((spots, LANES), f32),
         vmem((spots, LANES), f32),
         vmem((spots, LANES), f32),
         vmem((8, LANES), f32),
-        vmem((5, 8, LANES), f32),
+        vmem((8, LANES), f32),
         vmem((NCH, spots, width), bf16),
         vmem((NCH, spots, width), bf16),
         vmem((n_cells, LANES), f32),
@@ -799,10 +751,10 @@
         vmem((NCH, 4, 24, LANES), f32),
         vmem((NCH, 4, 24, LANES), f32),
         vmem((NCH, 2, 24, LANES), f32),
-        vmem((2, 8, LANES), f32),
-        vmem((2, 8, LANES), f32),
-        vmem((2, 4, 8, LANES), f32),
-        vmem((2, 4, 8, LANES), f32),
+        vmem((3, 8, LANES), f32),
+        vmem((3, 8, LANES), f32),
+        vmem((3, 4, 8, LANES), f32),
+        vmem((3, 4, 8, LANES), f32),
         vmem((NCH, 2) + ring, f32),
         vmem((NCH, 2, 4, 2, 2, 16, LANES), f32),
         vmem((NCH, 2, 4, 2, 2, 16, LANES), f32),
@@ -811,26 +763,22 @@
         vmem((NCH, 2, 4, 16, LANES), f32),
         vmem((NCH, 2, 4, 16, LANES), f32),
         vmem((NCH, 3, 2, 16, LANES), f32),
-        dma((NCH, 2)), dma((NCH,)), dma((tiles,)),
+        dma((1,)), dma((NCH,)), dma((tiles,)),
         dma((NCH, 3)), dma((NCH, 3)), dma((NCH, 2)), dma((NCH, 2)), dma((NCH, 2)), dma((NCH, 2)), dma((NCH,)), dma((NCH,)),
-        dma((3,)), dma((3,)), dma((1,)), dma((1,)), dma((1,)), dma((1,)), dma((1,)), dma((1,)),
         dma((NCH,)), dma((NCH,)), dma((NCH, 3)), dma((NCH, 3)), dma((NCH, 3)), dma((NCH, 3)), dma((NCH,)), dma((NCH,)),
-        dma((2,)), dma((2,)), dma((2, 3)), dma((2, 3)), dma((2, 3)), dma((2, 3)),
+        dma((3,)), dma((3,)), dma((3, 3)), dma((3, 3)), dma((3, 3)), dma((3, 3)),
         dma((NCH,)), dma((NCH,)), dma((NCH, 2)), dma((NCH, 2)), dma((NCH, 2)), dma((NCH, 2)), dma((NCH, 3)), dma((NCH, 3)),
     ]
     mask = cell_mask.reshape(n_cells // LANES, LANES)
     held = (
         vmem((NCH, spots // BR, BR, width), f32),
         vmem((tiles, n_cells, LANES), f32),
-        vmem((tiles, n_cells, LANES), f32),
-        vmem((n_cells, LANES), f32),
-        vmem((tiles, LANES), f32),
-        vmem((8, width), f32),
+        vmem((8, LANES), f32),
         vmem((8, LANES), f32),
         vmem((8, LANES), f32),
         vmem((n_slides, genes), f32),
         vmem((tiles, LANES), f32),
-        vmem((1, LANES), f32),
+        vmem((1, own), f32),
         vmem((own, genes), f32),
     )
     between = pl.pallas_call(
@@ -859,8 +807,8 @@
             jax.ShapeDtypeStruct((own, genes), f32),
         ),
         in_specs=[inside] * (len(held) + 1),
-        out_specs=(scalars, scalars, anywhere, inside, inside, anywhere, inside, inside),
-        scratch_shapes=[dma((NCH,)), dma((tiles,))],
+        out_specs=(anywhere,) * 8,
+        scratch_shapes=[pltpu.SMEM((3,), f32), pltpu.SMEM((4,), f32), dma((NCH,)), dma((tiles,)), dma((6,))],
         compiler_params=pltpu.CompilerParams(vmem_limit_bytes=24 << 20),
     )(*between, mask)
     terms, reg, pred, gcos, scos, glog, gfilt, gcell = out

time: 82.3 us -> 79.3 us (0.964)
  Pallas kernels: 81.5 us -> 78.4 us
    pallas_call x1, Pallas kernels: 76.7 us -> 74.2 us  [fused(): pl.pallas_call(fused_kernel, out_shape=held, in_specs=[anywhere, scalars,...]
where the time goes in v3:
time: 79.3 us; the launch traced here: 79.1 us
  Pallas kernels  78.4 us (99%)
    pallas_call x1, Pallas kernels, fused(): pl.pallas_call(fused_kernel, out_shape=held, in_specs=[anywhere, scalars,...  74.2 us
    pallas_call x1, Pallas kernels, fused(): pl.pallas_call(finish_kernel, out_shape=(jax.ShapeDtypeStruct((3,), f32),...  4.21 us

profile of v3, /device:TPU:0, one launch (start us, length us, event | category | flops | bytes accessed | tf_op | source)
XLA Modules:
  0.0 79.1 jit_solution(11012414403280095233)
XLA Ops:
  0.6 0.0 copy-start
  0.6 74.2 %shard_map.143 = (f32[8,32,32,256]{3,2,1,0:T(8,128)S(1)}, f32[8,512,128]{2,1,0:T(8,128)S(1)}, f32[8,128]{1,0:T(8,128)S(1)}, f32[8,128]{1,0:T(8,128)S(1)}, f32[8,...) custom-call(f32[512,1024]{1,0:T(8,128)} %logits_hbm.1, ...), custom_call_target="tpu_custom_call" | custom-call | tf_op jit(solution)/shard_map/pallas_call | solution.py:784
  74.9 0.0 copy-done
  74.9 4.2 %shard_map.144 = (f32[3]{0:T(128)}, f32[4]{0:T(128)}, f32[32,32,2048]{2,1,0:T(8,128)}, f32[8,2048]{1,0:T(8,128)}, f32[8,128]{1,0:T(8,128)}, /*index=5*/f32[512,1...) custom-call(f32[8,32,32,256]{3,2,1,0:T(8,128)S(1)} %get-tuple-element.25.pv, f32[8,512,128]{2,1,0:T(8,128)S(1)} %get-tuple-element.26.gw, ...), custom_call_target="tpu_custom_call" | custom-call | tf_op jit(solution)/shard_map/pallas_call | solution.py:797
Async XLA Ops:
  0.6 74.2 %copy-start = (s32[512]{0:T(512)S(1)}, s32[512]{0:T(512)}, u32[]{:S(2)}) copy-start(s32[512]{0:T(512)} %param.11) | copy-start | bytes 6148

commit v4 on v3

--- a/solution.py
+++ b/solution.py
@@ -408,19 +408,21 @@
     lax.fori_loop(6, NCH, target_sums, 0)
     stage_z(4)
     leave_z(AHEAD + 4)
-    stage_2(0)
     stage_1(2)
     slide_sums()
+    stage_z(5)
+    stage_2(0)
+    stage_1(3)
 
     def gather_tick(t, _):
-        c = t - 5
+        c = t - 6
         pl.when(t < NCH)(lambda: stage_z(t))
         pl.when(t + AHEAD < NCH)(lambda: leave_z(t + AHEAD))
-        pl.when(t - 4 < NCH)(lambda: stage_2(t - 4))
-        pl.when(t - 2 < NCH)(lambda: stage_1(t - 2))
+        pl.when(t - 5 < NCH)(lambda: stage_2(t - 5))
         predict(c)
         predicted_sums(c)
         b1(c).start()
+        pl.when(t - 2 < NCH)(lambda: stage_1(t - 2))
         pl.when(c == 0)(lambda: vector_second(0))
         pl.when(c == 2)(lambda: vector_third(0))
         pl.when(c >= 1)(lambda: sum_second(c - 1))
@@ -428,7 +430,7 @@
         pl.when(c >= 6)(lambda: sum_fourth(c - 6))
         return 0
 
-    lax.fori_loop(5, NCH + 5, gather_tick, 0)
+    lax.fori_loop(6, NCH + 6, gather_tick, 0)
 
     lane128 = lax.broadcasted_iota(jnp.int32, (LANES, LANES), 1)
     slide_of_lane = lax.rem(lane128, 8).astype(f32)
@@ -545,11 +547,11 @@
             gw[i] = prob * (grad - jnp.sum(prob * grad, axis=0, keepdims=True))
 
     def back_tick(t, _):
-        pl.when(t >= 3)(lambda: sc2(t - 3))
         pl.when(t < last)(lambda: sum_last(t + 1))
         backward(t)
         pl.when(t >= 1)(lambda: sc1(t - 1))
-        pl.when(t >= 4)(lambda: sc3(t - 4))
+        pl.when(t >= 3)(lambda: sc2(t - 3))
+        pl.when(t >= 5)(lambda: sc3(t - 5))
         pl.when(t <= 1)(lambda: sum_third(last - 1 + t))
         pl.when(t <= 4)(lambda: sum_fourth(last - 4 + t))
 
@@ -565,7 +567,6 @@
         def _():
             vector_third(1)
 
-        pl.when(t >= 6)(lambda: sc4(t - 6))
         return 0
 
     def slide_totals():
@@ -595,18 +596,22 @@
     sum_last(0)
     gene_coefs(0)
     lax.fori_loop(0, NCH, back_tick, 0)
-    sc1(last)
-    sc3(last - 3)
-    sc2(last - 2)
+    sc1(7)
+    sc2(5)
+    sc3(3)
     spot_part(0)
-    sc3(last - 2)
-    sc2(last - 1)
-    sc2(last)
+    sc2(6)
+    sc3(4)
+    sc2(7)
+    sc3(5)
     spot_part(1)
-    sc3(last - 1)
-    sc3(last)
-    for c in range(NCH - 6, NCH - 3):
-        sc4(c)
+    sc3(6)
+    sc3(7)
+    sc4(0)
+    sc4(1)
+    sc4(2)
+    sc4(3)
+    sc4(4)
     spot_part(2)
     spot_part(3)
 
@@ -624,18 +629,12 @@
 
     keep = own_lanes(keep)
     rest = own_lanes(rest)
-    for c in range(NCH - 3, NCH):
-        sc4(c)
-    genes_part = jnp.concatenate([along[...], jnp.zeros((LANES - 16, LANES), f32)], axis=0)
-    genes_part = jnp.sum(genes_part.T, axis=0, keepdims=True)
-    gfilt_ref[...] = ((genes_part + rest) * keep * (1.0 - keep))[:, : gfilt_ref.shape[1]]
 
     def leave(c, _):
         for k in range(3):
             z_out(c, k).wait_send()
             b2_out(c, k).wait_send()
             b3_out(c, k).wait_send()
-            scatter_z(c, k).wait_send()
         for d in s1_out(c) + s2_out(c) + scatter_one(c) + scatter_two(c):
             d.wait_send()
         s3_out(c).wait_send()
@@ -645,11 +644,23 @@
         return 0
 
     lax.fori_loop(0, NCH, leave, 0)
+    for c in range(NCH - 3):
+        for k in range(3):
+            scatter_z(c, k).wait_send()
     for n in range(3):
         v1(n).wait_send()
         for k in range(3):
             v2(n, here, k).wait_send()
             v3(n, z, k).wait_send()
+    for c in range(NCH - 3, NCH):
+        sc4(c)
+    genes_part = jnp.concatenate([along[...], jnp.zeros((LANES - 16, LANES), f32)], axis=0)
+    genes_part = jnp.sum(genes_part.T, axis=0, keepdims=True)
+    gfilt_ref[...] = ((genes_part + rest) * keep * (1.0 - keep))[:, : gfilt_ref.shape[1]]
+
+    for c in range(NCH - 3, NCH):
+        for k in range(3):
+            scatter_z(c, k).wait_send()
 
 
 def finish_kernel(

time: 79.3 us -> 76.2 us (0.961)
  Pallas kernels: 78.4 us -> 75.4 us
    pallas_call x1, Pallas kernels: 74.2 us -> 71.2 us  [fused(): pl.pallas_call(fused_kernel, out_shape=held, in_specs=[anywhere, scalars,...]
where the time goes in v4:
time: 76.2 us; the launch traced here: 76.1 us
  Pallas kernels  75.4 us (99%)
    pallas_call x1, Pallas kernels, fused(): pl.pallas_call(fused_kernel, out_shape=held, in_specs=[anywhere, scalars,...  71.2 us
    pallas_call x1, Pallas kernels, fused(): pl.pallas_call(finish_kernel, out_shape=(jax.ShapeDtypeStruct((3,), f32),...  4.21 us

profile of v4, /device:TPU:0, one launch (start us, length us, event | category | flops | bytes accessed | tf_op | source)
XLA Modules:
  0.0 76.1 jit_solution(1794909749640624801)
XLA Ops:
  0.6 0.0 copy-start
  0.6 71.2 %shard_map.143 = (f32[8,32,32,256]{3,2,1,0:T(8,128)S(1)}, f32[8,512,128]{2,1,0:T(8,128)S(1)}, f32[8,128]{1,0:T(8,128)S(1)}, f32[8,128]{1,0:T(8,128)S(1)}, f32[8,...) custom-call(f32[512,1024]{1,0:T(8,128)} %logits_hbm.1, ...), custom_call_target="tpu_custom_call" | custom-call | tf_op jit(solution)/shard_map/pallas_call | solution.py:795
  71.9 0.0 copy-done
  71.9 4.2 %shard_map.144 = (f32[3]{0:T(128)}, f32[4]{0:T(128)}, f32[32,32,2048]{2,1,0:T(8,128)}, f32[8,2048]{1,0:T(8,128)}, f32[8,128]{1,0:T(8,128)}, /*index=5*/f32[512,1...) custom-call(f32[8,32,32,256]{3,2,1,0:T(8,128)S(1)} %get-tuple-element.25.pv, f32[8,512,128]{2,1,0:T(8,128)S(1)} %get-tuple-element.26.gw, ...), custom_call_target="tpu_custom_call" | custom-call | tf_op jit(solution)/shard_map/pallas_call | solution.py:808
Async XLA Ops:
  0.6 71.2 %copy-start = (s32[512]{0:T(512)S(1)}, s32[512]{0:T(512)}, u32[]{:S(2)}) copy-start(s32[512]{0:T(512)} %param.11) | copy-start | bytes 6148

commit v5 on v4

--- a/solution.py
+++ b/solution.py
@@ -99,13 +99,23 @@
     own_keep = jax.nn.sigmoid(mine)
     ownk[...] = own_keep
     along[...] = jnp.zeros_like(along)
+    def one_hot(i, _):
+        ids = ids_ref[pl.ds(i, 1), :]
+        square = (lax.broadcasted_iota(jnp.int32, (LANES, LANES), 0) == ids).astype(f32)
+        oh[lanes(i), :] = square.T.astype(bf16)
+        per = LANES // BR
+        turned = jnp.broadcast_to(ids, (LANES, LANES)).astype(f32).T
+        idc[pl.ds(i * per, per)] = turned.reshape(per, BR, LANES)
+        return 0
+
+    lax.fori_loop(0, tiles, one_hot, 0)
+    for q in range(n_cells // LANES):
+        line = mask_ref[q : q + 1, :].astype(f32)
+        valid[q * LANES : (q + 1) * LANES, :] = jnp.broadcast_to(line, (LANES, LANES)).T
     own_cells.wait()
     for c in range(NCH):
         for h in range(2):
             buf[c, h, z, y, x, core] = own_keep * ownc[:, (c * 2 + h) * LANES : (c * 2 + h + 1) * LANES]
-    for q in range(n_cells // LANES):
-        line = mask_ref[q : q + 1, :].astype(f32)
-        valid[q * LANES : (q + 1) * LANES, :] = jnp.broadcast_to(line, (LANES, LANES)).T
     pl.semaphore_wait(barrier, 7)
 
     def z_out(c, k):
@@ -236,15 +246,6 @@
         tlo[lanes(i), :] = low
         return ent + jnp.sum(prob * (value - top - jnp.log(total)), axis=0, keepdims=True)
 
-    def one_hot(i, _):
-        ids = ids_ref[pl.ds(i, 1), :]
-        square = (lax.broadcasted_iota(jnp.int32, (LANES, LANES), 0) == ids).astype(f32)
-        oh[lanes(i), :] = square.T.astype(bf16)
-        per = LANES // BR
-        turned = jnp.broadcast_to(ids, (LANES, LANES)).astype(f32).T
-        idc[pl.ds(i * per, per)] = turned.reshape(per, BR, LANES)
-        return 0
-
     def leave_z(c):
         for k in range(3):
             z_out(c, k).start()
@@ -260,10 +261,9 @@
             d.start()
 
     def stage_1(c):
-        for d in s1_in(c):
-            d.wait_recv()
-        for d in s2_out(c):
-            d.start()
+        for arrived, onward in zip(s1_in(c), s2_out(c)):
+            arrived.wait_recv()
+            onward.start()
 
     def stage_2(c):
         for d in s2_in(c):
@@ -287,7 +287,6 @@
     sd[...] = jnp.zeros_like(sd)
     sp[...] = jnp.zeros_like(sp)
     st[...] = jnp.zeros_like(st)
-    lax.fori_loop(0, tiles, one_hot, 0)
 
     begins = [jnp.sum((ids_ref[...] < k).astype(jnp.int32)) for k in range(n_slides + 1)]
     firsts = [jnp.minimum(lax.div(begins[k], BR), n_blocks - 1) for k in range(n_slides)]
@@ -478,12 +477,13 @@
             d.start()
 
     def sc2(c):
-        for d in scatter_one(c):
-            d.wait_recv()
+        arrived, onward = scatter_one(c), scatter_two(c)
+        arrived[0].wait_recv()
         tt_[c, 0] = sb[c, 0, :, y] + r1[c, 0]
+        onward[0].start()
+        arrived[1].wait_recv()
         tt_[c, 1] = sb[c, 1, :, :, x] + r1[c, 1]
-        for d in scatter_two(c):
-            d.start()
+        onward[1].start()
 
     def sc3(c):
         for d in scatter_two(c):
@@ -530,8 +530,8 @@
         out = mm(jnp.concatenate([wh, wl, wh], axis=1), jnp.concatenate([gh, gh, gl], axis=0))
         for h in range(2):
             part[c, h] = out[:, h * LANES : (h + 1) * LANES].reshape(4, 2, 2, 2, 16, LANES)
+        scatter_sib(c).start()
         gene_coefs(jnp.minimum(c + 1, last))
-        scatter_sib(c).start()
 
     def spot_part(n):
         at = pl.ds(n * GR, GR)

time: 76.2 us -> 76 us (level)
  no operation moved by 1% of the time
where the time goes in v5:
time: 76 us; the launch traced here: 75.9 us
  Pallas kernels  75.2 us (99%)
    pallas_call x1, Pallas kernels, fused(): pl.pallas_call(fused_kernel, out_shape=held, in_specs=[anywhere, scalars,...  71 us
    pallas_call x1, Pallas kernels, fused(): pl.pallas_call(finish_kernel, out_shape=(jax.ShapeDtypeStruct((3,), f32),...  4.21 us

profile of v5, /device:TPU:0, one launch (start us, length us, event | category | flops | bytes accessed | tf_op | source)
XLA Modules:
  0.0 75.9 jit_solution(14096244213926837824)
XLA Ops:
  0.6 0.0 copy-start
  0.6 71.0 %shard_map.143 = (f32[8,32,32,256]{3,2,1,0:T(8,128)S(1)}, f32[8,512,128]{2,1,0:T(8,128)S(1)}, f32[8,128]{1,0:T(8,128)S(1)}, f32[8,128]{1,0:T(8,128)S(1)}, f32[8,...) custom-call(f32[512,1024]{1,0:T(8,128)} %logits_hbm.1, ...), custom_call_target="tpu_custom_call" | custom-call | tf_op jit(solution)/shard_map/pallas_call | solution.py:795
  71.6 0.0 copy-done
  71.7 4.2 %shard_map.144 = (f32[3]{0:T(128)}, f32[4]{0:T(128)}, f32[32,32,2048]{2,1,0:T(8,128)}, f32[8,2048]{1,0:T(8,128)}, f32[8,128]{1,0:T(8,128)}, /*index=5*/f32[512,1...) custom-call(f32[8,32,32,256]{3,2,1,0:T(8,128)S(1)} %get-tuple-element.25.pv, f32[8,512,128]{2,1,0:T(8,128)S(1)} %get-tuple-element.26.gw, ...), custom_call_target="tpu_custom_call" | custom-call | tf_op jit(solution)/shard_map/pallas_call | solution.py:808
Async XLA Ops:
  0.6 71.0 %copy-start = (s32[512]{0:T(512)S(1)}, s32[512]{0:T(512)}, u32[]{:S(2)}) copy-start(s32[512]{0:T(512)} %param.11) | copy-start | bytes 6148

commit v6 on v5

--- a/solution.py
+++ b/solution.py
@@ -349,7 +349,6 @@
         return 0
 
     def predict(c):
-        s3_in(c).wait_recv()
         whole = jnp.concatenate([buf[c, h].reshape(n_cells, LANES) for h in range(2)], axis=1)
         high, low = split(whole)
         chi[c] = high
@@ -357,10 +356,6 @@
         wh, wl = thi[...], tlo[...]
         pred = mm(jnp.concatenate([wh, wl, wh], axis=1), jnp.concatenate([high, high, low], axis=0))
         pv[c] = pred.reshape(n_blocks, BR, width)
-
-    def predicted_sums(c):
-        by_rows(c, of_both, (sd, sp))
-        gene_sums(c, of_both, 2, 0)
 
     def slide_sums():
         keep_rows = jax.nn.sigmoid(vector_last(2))
@@ -416,20 +411,29 @@
     def gather_tick(t, _):
         c = t - 6
         pl.when(t < NCH)(lambda: stage_z(t))
-        pl.when(t + AHEAD < NCH)(lambda: leave_z(t + AHEAD))
         pl.when(t - 5 < NCH)(lambda: stage_2(t - 5))
+        s3_in(c).wait_recv()
+        gene_sums(c - 1, of_both, 2, 0)
+        b1(c - 1).start()
         predict(c)
-        predicted_sums(c)
-        b1(c).start()
+        by_rows(c, of_both, (sd, sp))
         pl.when(t - 2 < NCH)(lambda: stage_1(t - 2))
-        pl.when(c == 0)(lambda: vector_second(0))
         pl.when(c == 2)(lambda: vector_third(0))
-        pl.when(c >= 1)(lambda: sum_second(c - 1))
+        sum_second(c - 1)
         pl.when(c >= 3)(lambda: sum_third(c - 3))
         pl.when(c >= 6)(lambda: sum_fourth(c - 6))
         return 0
 
-    lax.fori_loop(6, NCH + 6, gather_tick, 0)
+    stage_z(6)
+    stage_2(1)
+    s3_in(0).wait_recv()
+    predict(0)
+    by_rows(0, of_both, (sd, sp))
+    stage_1(4)
+    vector_second(0)
+    lax.fori_loop(7, NCH + 6, gather_tick, 0)
+    gene_sums(last, of_both, 2, 0)
+    b1(last).start()
 
     lane128 = lax.broadcasted_iota(jnp.int32, (LANES, LANES), 1)
     slide_of_lane = lax.rem(lane128, 8).astype(f32)
@@ -547,25 +551,13 @@
             gw[i] = prob * (grad - jnp.sum(prob * grad, axis=0, keepdims=True))
 
     def back_tick(t, _):
+        pl.when(t >= 4)(lambda: sc2(t - 4))
         pl.when(t < last)(lambda: sum_last(t + 1))
         backward(t)
         pl.when(t >= 1)(lambda: sc1(t - 1))
-        pl.when(t >= 3)(lambda: sc2(t - 3))
         pl.when(t >= 5)(lambda: sc3(t - 5))
         pl.when(t <= 1)(lambda: sum_third(last - 1 + t))
         pl.when(t <= 4)(lambda: sum_fourth(last - 4 + t))
-
-        @pl.when(t == 4)
-        def _():
-            slide_totals()
-
-        @pl.when(t == 5)
-        def _():
-            vector_second(1)
-
-        @pl.when(t == 7)
-        def _():
-            vector_third(1)
 
         return 0
 
@@ -596,15 +588,19 @@
     sum_last(0)
     gene_coefs(0)
     lax.fori_loop(0, NCH, back_tick, 0)
+    slide_totals()
     sc1(7)
+    sc2(4)
     sc2(5)
     sc3(3)
     spot_part(0)
+    vector_second(1)
     sc2(6)
     sc3(4)
     sc2(7)
     sc3(5)
     spot_part(1)
+    vector_third(1)
     sc3(6)
     sc3(7)
     sc4(0)

time: 76 us -> 75.8 us (level)
  no operation moved by 1% of the time
where the time goes in v6:
time: 75.8 us; the launch traced here: 75.7 us
  Pallas kernels  75 us (99%)
    pallas_call x1, Pallas kernels, fused(): pl.pallas_call(fused_kernel, out_shape=held, in_specs=[anywhere, scalars,...  70.8 us
    pallas_call x1, Pallas kernels, fused(): pl.pallas_call(finish_kernel, out_shape=(jax.ShapeDtypeStruct((3,), f32),...  4.21 us

profile of v6, /device:TPU:0, one launch (start us, length us, event | category | flops | bytes accessed | tf_op | source)
XLA Modules:
  0.0 75.7 jit_solution(15386664547507002979)
XLA Ops:
  0.6 0.0 copy-start
  0.6 70.8 %shard_map.143 = (f32[8,32,32,256]{3,2,1,0:T(8,128)S(1)}, f32[8,512,128]{2,1,0:T(8,128)S(1)}, f32[8,128]{1,0:T(8,128)S(1)}, f32[8,128]{1,0:T(8,128)S(1)}, f32[8,...) custom-call(f32[512,1024]{1,0:T(8,128)} %logits_hbm.1, ...), custom_call_target="tpu_custom_call" | custom-call | tf_op jit(solution)/shard_map/pallas_call | solution.py:791
  71.4 0.0 copy-done
  71.5 4.2 %shard_map.144 = (f32[3]{0:T(128)}, f32[4]{0:T(128)}, f32[32,32,2048]{2,1,0:T(8,128)}, f32[8,2048]{1,0:T(8,128)}, f32[8,128]{1,0:T(8,128)}, /*index=5*/f32[512,1...) custom-call(f32[8,32,32,256]{3,2,1,0:T(8,128)S(1)} %get-tuple-element.25.pv, f32[8,512,128]{2,1,0:T(8,128)S(1)} %get-tuple-element.26.gw, ...), custom_call_target="tpu_custom_call" | custom-call | tf_op jit(solution)/shard_map/pallas_call | solution.py:804
Async XLA Ops:
  0.6 70.8 %copy-start = (s32[512]{0:T(512)S(1)}, s32[512]{0:T(512)}, u32[]{:S(2)}) copy-start(s32[512]{0:T(512)} %param.11) | copy-start | bytes 6148
